TPU v7x, 128 devices: a whole 4x4x4 slice. The times are simulated.
128 devices in a mesh: img: 8 (over z_hi, x), sp: 16 (over y, z_lo, core).
Axes of the slice: x: 4, y: 4, z: 4 (z_hi: 2, z_lo: 2; z = z_hi * 2 + z_lo), core: 2. Of those that a mesh axis runs over, the one named last changes fastest.
Arguments:
- tokens: bfloat16 [8, 14336, 2240], P('img', 'sp'), may hold values from -12 to 12
- queries: bfloat16 [8, 14336, 1120], P('img', 'sp'), may hold values from -6 to 6
- w_key: bfloat16 [2240, 1120], P('img'), may hold values from -0.125 to 0.125
- w_value: bfloat16 [2240, 1120], P('img'), may hold values from -0.125 to 0.125
- cotangent: bfloat16 [8, 14336, 1120], P('img', 'sp'), may hold values from -6 to 6
Outputs:
- attended: bfloat16 [8, 14336, 1120], P('img', 'sp')
- d_tokens: bfloat16 [8, 14336, 2240], P('img', 'sp')
- d_queries: bfloat16 [8, 14336, 1120], P('img', 'sp')
- d_w_key: float32 [2240, 1120], P('img')
- d_w_value: float32 [2240, 1120], P('img')
All inputs are finite; a program needn't handle non-finite values.
Results may differ from a plain program's by a relative error of at most 0.006.
Values may be sent and summed in bfloat16 or wider, within the bound.
A program may use at most 128 MiB of HBM per device.

v0:
```python
import jax
import jax.numpy as jnp
from jax import lax
from jax.sharding import PartitionSpec as P

HD = 32


EPS_DEN = 1e-06


def sent_together(arrays, axis, dim, along):
    ends, at = ([], 0)
    for a in arrays[:-1]:
        at += a.shape[along]
        ends.append(at)
    both = jnp.concatenate(arrays, axis=along)
    return tuple(jnp.split(lax.all_gather(both, axis, axis=dim, tiled=True), ends, axis=along))


def from_everyone(value, axis):
    peers = lax.axis_size(axis)
    return lax.all_to_all(
        jnp.broadcast_to(value[None], (peers, *value.shape)), axis, 0, 0, tiled=True
    )


def over_copies(value, axis):
    return from_everyone(value, axis).sum(axis=0)


def in_one(arrays, axis):
    ends = [0]
    for a in arrays:
        ends.append(ends[-1] + a.size)
    subtotal = over_copies(jnp.concatenate([a.ravel() for a in arrays]), axis)
    return tuple((subtotal[b:e].reshape(a.shape) for a, b, e in zip(arrays, ends, ends[1:])))


def cut_along(value, dim, peers):
    dims = value.shape
    pieces = value.reshape(*dims[:dim], peers, dims[dim] // peers, *dims[dim + 1 :])
    return jnp.moveaxis(pieces, dim, 0)


def sum_at_owner(value, axis, dim):
    pieces = cut_along(value, dim, lax.axis_size(axis))
    arrived = lax.all_to_all(pieces, axis, split_axis=0, concat_axis=0, tiled=True)
    return arrived.sum(axis=0)


def body(tokens, queries, w_key, w_value, cotangent):
    high = lax.Precision.HIGHEST
    tok_rows = tokens[0]
    count = tok_rows.shape[0]
    width = w_key.shape[1]
    heads = width // HD
    tok_img = count * lax.axis_size("sp")
    images = lax.axis_size("img")
    gathered = sent_together((w_key, w_value), "img", 0, 1)
    key_pre = jnp.dot(tok_rows, gathered[0], preferred_element_type=jnp.float32)
    val_pre = jnp.dot(tok_rows, gathered[1], preferred_element_type=jnp.float32)
    key_feat = jnp.maximum(key_pre, 0.0).astype(jnp.bfloat16).reshape(count, heads, HD)
    val_feat = val_pre.astype(jnp.bfloat16).reshape(count, heads, HD)
    state_part = jnp.einsum("thi,thj->hij", key_feat, val_feat, preferred_element_type=jnp.float32)
    norm_part = jnp.sum(key_feat, axis=0, dtype=jnp.float32)
    kv_state, key_norm = in_one((state_part, norm_part), "sp")
    q_feat = jnp.maximum(queries[0].astype(jnp.float32), 0.0).reshape(count, heads, HD)
    numerator = jnp.einsum("thi,hij->thj", q_feat, kv_state, precision=high)
    denominator = jnp.einsum("thi,hi->th", q_feat, key_norm, precision=high) + EPS_DEN
    attn_f32 = numerator / denominator[..., None]
    attended = attn_f32.astype(jnp.bfloat16).reshape(1, count, width)
    cot_f32 = cotangent[0].astype(jnp.float32).reshape(count, heads, HD)
    d_num = cot_f32 / denominator[..., None]
    d_den = -jnp.sum(cot_f32 * attn_f32, axis=-1) / denominator
    d_feat = (
        jnp.einsum("thj,hij->thi", d_num, kv_state, precision=high)
        + d_den[..., None] * key_norm[None]
    )
    d_queries = jnp.where(q_feat > 0, d_feat, 0.0).astype(jnp.bfloat16).reshape(1, count, width)
    grad_part = jnp.einsum("thi,thj->hij", q_feat, d_num, precision=high)
    gnorm_part = jnp.einsum("th,thi->hi", d_den, q_feat, precision=high)
    grad_state, grad_norm = in_one((grad_part, gnorm_part), "sp")
    grad_state = grad_state * tok_img
    grad_norm = grad_norm * tok_img
    key_f32 = key_feat.astype(jnp.float32)
    d_key_f = (
        jnp.einsum("thj,hij->thi", val_feat.astype(jnp.float32), grad_state, precision=high)
        + grad_norm[None]
    )
    d_key = jnp.where(key_f32 > 0, d_key_f, 0.0).astype(jnp.bfloat16).reshape(count, width)
    d_value = (
        jnp.einsum("thi,hij->thj", key_f32, grad_state, precision=high)
        .astype(jnp.bfloat16)
        .reshape(count, width)
    )
    back_dims = (((1,), (1,)), ((), ()))
    d_flat = lax.dot_general(
        d_key, gathered[0], back_dims, preferred_element_type=jnp.float32
    ) + lax.dot_general(d_value, gathered[1], back_dims, preferred_element_type=jnp.float32)
    d_tokens = d_flat.astype(jnp.bfloat16).reshape(1, count, tok_rows.shape[1])
    d_both = jnp.concatenate([d_key, d_value], axis=1)
    tok_dims = (((0,), (0,)), ((), ()))
    grad_term = lax.dot_general(tok_rows, d_both, tok_dims, preferred_element_type=jnp.float32)
    col_sums = lax.psum_scatter(grad_term, "sp", scatter_dimension=1, tiled=True)
    row_sums = sum_at_owner(col_sums, "img", 0)
    grad_whole = lax.all_gather(row_sums, "sp", axis=1, tiled=True)
    scale = 1.0 / jnp.sqrt(jnp.float32(images * tok_img))
    grad_whole = grad_whole * scale
    return (attended, d_tokens, d_queries, grad_whole[:, :width], grad_whole[:, width:])


def solution(mesh):
    in_specs = (
        P("img", "sp", None),
        P("img", "sp", None),
        P("img", None),
        P("img", None),
        P("img", "sp", None),
    )
    out_specs = (
        P("img", "sp", None),
        P("img", "sp", None),
        P("img", "sp", None),
        P("img", None),
        P("img", None),
    )
    return jax.shard_map(body, mesh=mesh, in_specs=in_specs, out_specs=out_specs, check_vma=False)
```

profile of v0, /device:TPU:1, one launch (start us, length us, event | category | flops | bytes accessed | tf_op | source)
XLA Modules:
  0.0 602.5 jit_solution(1393491897490882497)
XLA Ops:
  7.2 2.6 pad_maximum_fusion
  9.9 129.7 %all-gather.4.cloned.1.call-done = bf16[2240,2240]{1,0:T(8,128)(2,1)} async-done(((bf16[280,2240]{1,0:T(8,128)(2,1)}), bf16[2240,2240]{1,0:T(8,128)(2,1)}) %all-gather.4.cloned.1.call-update) | async-done | bytes 10035216 | tf_op jit(solution)/shard_map/all_gather | solution.py:18
  139.5 9.5 %convert_reduce_fusion = (f32[1120]{0:T(1024)S(1)}, bf16[1120,896]{1,0:T(8,128)(2,1)S(1)}) fusion(bf16[1,896,2240]{1,2,0:T(8,128)(2,1)} %param.5, bf16[2240,2240]{1,0:T(8,128)(2,1)} %all-gather.4.cloned.1.call-done), kind=kOutput, calls=%fused_computation.29 | convolution fusion | flops 4499782656 | bytes 11186560 | tf_op jit(solution)/shard_map/dot_general | solution.py:61
  149.0 6.0 fusion.27
  157.3 2.8 broadcast_in_dim.6
  160.1 5.8 all-to-all-start
  165.9 3.8 convert_maximum_fusion
  169.7 26.3 %all-to-all-done = f32[16,1,36960]{2,1,0:T(1,128)} async-done(((f32[16,1,36960]{2,1,0:T(1,128)}), f32[16,1,36960]{2,1,0:T(1,128)}, u32[]{:S(2)}, u32[]{:S(2)}) %all-to-all-start) | async-done | bytes 2365472 | tf_op jit(solution)/shard_map/all_to_all | solution.py:23
  196.0 3.2 reduce_sum.46
  199.2 4.3 fusion.42
  203.8 7.5 %fusion.33 = f32[35,32,32]{2,1,0:T(8,128)S(1)} fusion(f32[896,35,32]{0,2,1:T(8,128)} %bitcast.85, bf16[896,35,32]{0,2,1:T(8,128)(2,1)} %bitcast.104, f32[896,35]{0,1:T(8,128)S(1)} %fusion.36), kind=kOutput, calls=%fused_computation.33 | convolution fusion | flops 387358720 | bytes 6289920 | tf_op jit(solution)/shard_map/thi,thj->hij/dot_general | solution.py:81
  211.4 6.7 %fusion.12 = (f32[896,35]{0,1:T(8,128)S(1)}, bf16[896,35,32]{0,2,1:T(8,128)(2,1)}) fusion(bf16[896,35,32]{0,2,1:T(8,128)(2,1)S(1)} %bitcast.106, f32[896,35]{0,1:T(8,128)S(1)} %fusion.36, f32[35,32,32]{2,1,0:T(8,128)S(1)} %reshape.110, f32[896,35,32]{0,2,1:T(8,128)S(1)} %bitcast.86), kind=kOutput, calls=%fused_computation.15 | convolution fusion | flops 390337920 | bytes 8422400 | tf_op jit(solution)/shard_map/thi,hij->thj/dot_general | solution.py:69
  218.1 3.9 fusion.37
  223.5 36.5 %all_to_all.17 = f32[16,1,36960]{2,1,0:T(1,128)} all-to-all(f32[16,1,36960]{2,1,0:T(1,128)S(1)} %broadcast_in_dim.7), channel_id=1, replica_groups=mesh['img'=8,'sp'=16] {'sp'}, dimensions={0} | all-to-all | bytes 4730880 | tf_op jit(solution)/shard_map/all_to_all | solution.py:23
  260.0 3.2 reduce_sum.48
  265.2 2.2 fusion.18
  268.8 14.4 %convolution_bitcast_fusion = f32[2240,2240]{0,1:T(8,128)} fusion(bf16[896,1120]{0,1:T(8,128)(2,1)S(1)} %bitcast.96, bf16[896,1120]{0,1:T(8,128)(2,1)S(1)} %bitcast.94, bf16[1,896,2240]{1,2,0:T(8,128)(2,1)S(1)} %copy-done.14), kind=kOutput, calls=%fused_computation | convolution fusion | flops 8999567360 | bytes 28098560 | tf_op jit(solution)/shard_map/dot_general | solution.py:104
  283.1 225.3 %fusion = f32[2240,144]{0,1:T(8,128)S(1)} fusion(f32[2240,2240]{0,1:T(8,128)} %convolution_bitcast_fusion), kind=kCustom, calls=%all-reduce-scatter | all-reduce-scatter fusion | flops 5160961 | bytes 21361152
  508.4 4.4 collective-permute-start
  514.1 5.6 collective-permute-done
  519.6 2.8 concatenate.16
  522.6 2.1 reshape.119
  524.7 1.9 copy.30
  526.7 23.2 %all_to_all.18 = f32[8,280,140]{1,2,0:T(8,128)} all-to-all(f32[8,280,140]{1,2,0:T(8,128)S(1)} %copy.30), channel_id=1, replica_groups=mesh['img'=8,'sp'=16] {'img'}, dimensions={0} | all-to-all | bytes 2508800 | tf_op jit(solution)/shard_map/all_to_all | solution.py:48
  549.9 2.3 reduce_sum.49
  553.0 7.5 %fusion.17 = bf16[896,35,32]{0,2,1:T(8,128)(2,1)} fusion(pred[896,35,32]{0,2,1:T(32,128)(4,1)S(1)} %bitcast.98, f32[35,32]{1,0:T(8,128)S(1)} %reshape.111, f32[896,35]{0,1:T(8,128)S(1)} %negate_divide_fusion, f32[35,32,32]{2,1,0:T(8,128)} %copy-done.8, bf16[896,35,32]{0,2,1:T(8,128)(2,1)} %bitcast.105, f32[896,35]{0,1:T(8,128)S(1)} %copy-done.10), kind=kOutput, calls=%fused_computation.21 | convolution fusion | flops 391372800 | bytes 5416320 | tf_op jit(solution)/shard_map/thj,hij->thi/dot_general | solution.py:77
  560.5 8.1 %fusion.5 = f32[896,2240]{0,1:T(8,128)S(1)} fusion(bf16[896,1120]{0,1:T(8,128)(2,1)S(1)} %bitcast.95, bf16[2240,2240]{1,0:T(8,128)(2,1)} %all-gather.4.cloned.1.call-done), kind=kOutput, calls=%fused_computation.10 | convolution fusion | flops 4495769600 | bytes 15196160 | tf_op jit(solution)/shard_map/dot_general | solution.py:98
  568.6 7.8 %fusion.1 = bf16[1,896,2240]{1,2,0:T(8,128)(2,1)} fusion(f32[896,2240]{0,1:T(8,128)S(1)} %fusion.5, bf16[896,1120]{0,1:T(8,128)(2,1)S(1)} %bitcast.97, bf16[2240,2240]{1,0:T(8,128)(2,1)S(1)} %bitcast.103), kind=kOutput, calls=%fused_computation.6 | convolution fusion | flops 4499783680 | bytes 19210240 | tf_op jit(solution)/shard_map/dot_general | solution.py:100
  576.4 9.5 %all-gather.6.cloned.1.call-done = f32[16,140,280]{2,1,0:T(8,128)} async-done(((f32[1,140,280]{2,1,0:T(8,128)}), f32[16,140,280]{2,1,0:T(8,128)}) %all-gather.6.cloned.1.call-update) | async-done | bytes 2508816 | tf_op jit(solution)/shard_map/all_gather | solution.py:107
  586.0 2.3 broadcast_multiply_fusion
  588.3 1.9 reshape.124
  590.2 2.2 fusion.40
  (69 shorter events, 12.2 us)
Async XLA Ops:
  7.2 132.4 %all-gather.4.cloned.1.call-start = ((), (), s32[]{:S(2)}) async-start(), calls=%async_computation.3 | async-start | bytes 11612160 | tf_op jit(solution)/shard_map/all_gather | solution.py:18
  139.5 9.5 %copy-start.12 = (bf16[2240,2240]{1,0:T(8,128)(2,1)S(1)}, bf16[2240,2240]{1,0:T(8,128)(2,1)}, u32[]{:S(2)}) copy-start(bf16[2240,2240]{1,0:T(8,128)(2,1)} %all-gather.4.cloned.1.call-done) | copy-start | bytes 30105604
  139.5 9.5 %copy-start.13 = (bf16[1,896,2240]{1,2,0:T(8,128)(2,1)S(1)}, bf16[1,896,2240]{1,2,0:T(8,128)(2,1)}, u32[]{:S(2)}) copy-start(bf16[1,896,2240]{1,2,0:T(8,128)(2,1)} %param.5) | copy-start | bytes 12042244
  155.0 1.3 copy-start.2
  160.1 35.9 %all-to-all-start = ((f32[16,1,36960]{2,1,0:T(1,128)}), f32[16,1,36960]{2,1,0:T(1,128)}, u32[]{:S(2)}, u32[]{:S(2)}) async-start(f32[16,1,36960]{2,1,0:T(1,128)} %broadcast_in_dim.6), calls=%async_computation | async-start | bytes 4734976 | tf_op jit(solution)/shard_map/all_to_all | solution.py:23
  165.9 420.1 %all-gather.6.cloned.1.call-start = ((), (), s32[]{:S(2)}) async-start(), calls=%async_computation.4 | async-start | bytes 3760128 | tf_op jit(solution)/shard_map/all_gather | solution.py:107
  203.6 7.8 %copy-start.9 = (f32[896,35]{0,1:T(8,128)}, f32[896,35]{0,1:T(8,128)S(1)}, u32[]{:S(2)}) copy-start(f32[896,35]{0,1:T(8,128)S(1)} %fusion.36) | copy-start | bytes 376324
  203.8 7.6 %copy-start.8 = (f32[35,32,32]{2,1,0:T(8,128)}, f32[35,32,32]{2,1,0:T(8,128)S(1)}, u32[]{:S(2)}) copy-start(f32[35,32,32]{2,1,0:T(8,128)S(1)} %reshape.110) | copy-start | bytes 430084
  203.8 7.6 %copy-start = (f32[1,896,1120]{1,2,0:T(8,128)S(1)}, f32[1,896,1120]{1,2,0:T(8,128)}, u32[]{:S(2)}) copy-start(f32[1,896,1120]{1,2,0:T(8,128)} %convert_maximum_fusion) | copy-start | bytes 12042244
  203.8 7.6 %copy-start.15 = (bf16[1,896,1120]{1,2,0:T(8,128)(2,1)S(1)}, bf16[1,896,1120]{1,2,0:T(8,128)(2,1)}, u32[]{:S(2)}) copy-start(bf16[1,896,1120]{1,2,0:T(8,128)(2,1)} %param.9) | copy-start | bytes 6021124
  263.4 1.8 copy-start.3
  265.2 2.3 copy-start.6
  265.2 3.5 copy-start.14
  267.5 1.3 copy-start.4
  283.1 229.7 %copy-start.11 = (u32[128]{0:T(128)S(1)}, u32[128]{0:T(128)}, u32[]{:S(2)}) copy-start(u32[128]{0:T(128)} %constant.16) | copy-start | bytes 1540
  508.4 11.2 %collective-permute-start = (f32[2240,60]{0,1:T(8,128)S(1)}, f32[2240,60]{0,1:T(8,128)}, u32[]{:S(2)}, u32[]{:S(2)}) collective-permute-start(f32[2240,60]{0,1:T(8,128)S(1)} %slice.48), channel_id=1, source_target_pairs={{0,1},{1,2},{2,3},{3,4},{4,5},{5,6},{6,7},{7,8},{8,9},{9,10},{10,1... | collective-permute-start | bytes 1612808
  524.7 27.5 %copy-start.1 = (bf16[1,896,1120]{1,2,0:T(8,128)(2,1)S(1)}, bf16[1,896,1120]{1,2,0:T(8,128)(2,1)}, u32[]{:S(2)}) copy-start(bf16[1,896,1120]{1,2,0:T(8,128)(2,1)} %param.6) | copy-start | bytes 6021124
  526.7 26.3 %copy-start.10 = (f32[896,35]{0,1:T(8,128)S(1)}, f32[896,35]{0,1:T(8,128)}, u32[]{:S(2)}) copy-start(f32[896,35]{0,1:T(8,128)} %copy-done.9) | copy-start | bytes 376324
  553.0 7.5 %copy-start.5 = (bf16[896,35,32]{0,2,1:T(8,128)(2,1)S(1)}, bf16[896,35,32]{0,2,1:T(8,128)(2,1)}, u32[]{:S(2)}) copy-start(bf16[896,35,32]{0,2,1:T(8,128)(2,1)} %copy-done.4) | copy-start | bytes 6021124
  553.0 15.6 %slice-start = ((s8[10321920]{0:T(1024)(128)(4,1)}), s8[4194304]{0:T(1024)(128)(4,1)S(1)}, s32[]{:S(2)}) async-start(s8[10321920]{0:T(1024)(128)(4,1)} %bitcast.102), calls=%async_computation.5 | async-start | bytes 8388608
  553.0 15.6 %slice-start.1 = ((s8[10321920]{0:T(1024)(128)(4,1)}), s8[4194304]{0:T(1024)(128)(4,1)S(1)}, s32[]{:S(2)}) async-start(s8[10321920]{0:T(1024)(128)(4,1)} %bitcast.102), calls=%async_computation.6 | async-start | bytes 8388608
  560.5 8.1 %copy-start.7 = (bf16[35,32,896]{2,1,0:T(8,128)(2,1)S(1)}, bf16[35,32,896]{2,1,0:T(8,128)(2,1)}, u32[]{:S(2)}) copy-start(bf16[35,32,896]{2,1,0:T(8,128)(2,1)} %copy-done.6) | copy-start | bytes 6021124
  560.5 8.1 %slice-start.2 = ((s8[10321920]{0:T(1024)(128)(4,1)}), s8[1933312]{0:T(1024)(128)(4,1)S(1)}, s32[]{:S(2)}) async-start(s8[10321920]{0:T(1024)(128)(4,1)} %bitcast.102), calls=%async_computation.7 | async-start | bytes 3866624
Sparse Core Ops, SparseCore 0:
  10.9 128.5 all-gather.3
  552.4 33.5 all-gather.5
where the time goes:
time: 612 us; the launch traced here: 603 us
  blocking collectives  285 us (47%)
  waiting for transfers between devices  171 us (28%)
  matrix products  80.4 us (13%)
  local copies, waits for them, and re-layouts  22.6 us (4%)
  other arithmetic  18 us (3%)
  between operations  15.3 us (2%)
  starting transfers between devices  10.2 us (2%)
    unnamed x1, blocking collectives  225 us
    all_gather x1, waiting for transfers between devices, sent_together(): lax.all_gather(both, axis, axis=dim, tiled=True)  130 us
    all_to_all x1, blocking collectives, from_everyone(): lax.all_to_all(jnp.broadcast_to(value[None], (peers, *value.shape)), axis...  36.5 us
    all_to_all x1, waiting for transfers between devices, from_everyone(): lax.all_to_all(jnp.broadcast_to(value[None], (peers, *value.shape)), axis...  26.3 us
    all_to_all x1, blocking collectives, sum_at_owner(): lax.all_to_all(pieces, axis, split_axis=0, concat_axis=0, tiled=True)  23.2 us
    dot_general x1, matrix products, body(): lax.dot_general(tok_rows, d_both, tok_dims, preferred_element_type=jnp.fl...  14.4 us
  transfers between devices with their start and end apart: 4, of which 4 were waited for; matrix products, arithmetic and copies ran while one was open for 5% of the time, Pallas kernels for 0%

commit v1 on v0

v1 whole, which is shorter than its diff:
```python
import jax
import jax.numpy as jnp
from jax import lax
from jax.experimental import pallas as pl
from jax.experimental.pallas import tpu as pltpu
from jax.sharding import PartitionSpec as P

HD = 32
EPS_DEN = 1e-06
BF = jnp.bfloat16
F32 = jnp.float32
MESH = pl.DeviceIdType.MESH
LANE = 128
VMEM_MAX = 64 * 1024 * 1024 - 65536
DMA = pltpu.SemaphoreType.DMA


def params(cid=None, sem=None):
    return pltpu.CompilerParams(
        collective_id=cid,
        has_side_effects=cid is not None,
        vmem_limit_bytes=VMEM_MAX,
        dimension_semantics=sem,
    )


class Seat:
    def __init__(self):
        img, sp = lax.axis_index("img"), lax.axis_index("sp")
        self.img, self.sp = img, sp
        self.zhi, self.x = img // 4, img % 4
        self.y, self.zlo, self.core = sp // 4, (sp // 2) % 2, sp % 2

    def at(self, dx=0, dy=0, hi=None, lo=None, core=None):
        x = (self.x + dx + 4) % 4
        y = (self.y + dy + 4) % 4
        hi = self.zhi if hi is None else hi
        lo = self.zlo if lo is None else lo
        core = self.core if core is None else core
        return {"img": hi * 4 + x, "sp": (y * 2 + lo) * 2 + core}

    def across(self):
        return self.at(hi=1 - self.zhi, lo=1 - self.zlo)

    def beside(self):
        return self.at(lo=1 - self.zlo)

    def partner(self):
        return self.at(core=1 - self.core)


def meet(devices):
    bar = pltpu.get_barrier_semaphore()
    for d in devices:
        pl.semaphore_signal(bar, inc=1, device_id=d, device_id_type=MESH)
    pl.semaphore_wait(bar, len(devices))


def remote(src, dst, ssem, rsem, device):
    return pltpu.make_async_remote_copy(
        src_ref=src, dst_ref=dst, send_sem=ssem, recv_sem=rsem, device_id=device, device_id_type=MESH
    )


HALVES = ((0, 144), (144, 136))
L0, L1, R0, R1, O0, O1, YL0, YR0, YO0, YL1, YR1, YO1, ZM0, ZM1, ZN0, ZN1 = range(16)


def gather_kernel(w_ref, tok_ref, out, tok_out, ssem, rsem, csem, lsem, tsem):
    s = Seat()
    m = s.y % 2
    right, left = s.at(dx=1), s.at(dx=-1)
    up, down = s.at(dy=1), s.at(dy=-1)
    partner, across = s.partner(), s.across()
    meet((right, left, up, down, partner, across))

    def part(mat, shard, h):
        return out.at[mat, shard, pl.ds(HALVES[h][0], HALVES[h][1])]

    def mine(mat, h):
        return w_ref.at[mat, pl.ds(HALVES[h][0], HALVES[h][1])]

    def place(k, core):
        hi = (s.zhi + core) % 2
        if k >= ZM0:
            return part(m if k < ZN0 else 1 - m, (1 - s.zhi) * 4 + s.x, (k - ZM0) % 2)
        dx, h = {
            L0: (3, 0), L1: (3, 1), R0: (1, 0), R1: (1, 1), O0: (2, 0), O1: (2, 1),
            YL0: (3, 0), YR0: (1, 0), YO0: (2, 0), YL1: (3, 1), YR1: (1, 1), YO1: (2, 1),
        }[k]
        return part(m if k < YL0 else 1 - m, hi * 4 + (s.x + dx) % 4, h)

    swap = remote(tok_ref, tok_out, tsem.at[0], tsem.at[1], partner)
    owns = [
        pltpu.make_async_copy(w_ref.at[i], out.at[i, s.img], lsem.at[i]) for i in range(2)
    ]
    sent = []

    def send(src, dst, k, device, sems, start=True):
        slot = len(sent)
        c = remote(src, dst, ssem.at[slot], sems.at[k], device)
        sent.append(c)
        if start:
            c.start()
        return c

    is0, is1 = s.core == 0, s.core == 1
    hi = (s.zhi + s.core) % 2
    seed = hi * 4 + s.x

    zs = [
        send(mine(mat, h), part(mat, s.img, h), k, across, rsem, False)
        for k, mat, h in ((ZM0, m, 0), (ZM1, m, 1), (ZN0, 1 - m, 0), (ZN1, 1 - m, 1))
    ]
    first = [
        (send(mine(m, h), part(m, s.img, h), k, d, rsem, False), h)
        for h, k, d in ((0, L0, right), (1, R1, left), (1, L1, right), (0, R0, left))
    ]
    second = [
        (remote(part(m, seed, h), part(m, seed, h), ssem.at[4 + i], rsem.at[k], d), h)
        for i, (h, k, d) in enumerate(((0, L0, right), (1, R1, left), (1, L1, right), (0, R0, left)))
    ]

    @pl.when(is1)
    def _():
        for c in zs:
            c.start()

    @pl.when(is0)
    def _():
        for c, _h in first:
            c.start()

    for c in owns:
        c.start()
    swap.start()

    def got(k, sems, core):
        ref = place(k, core)
        pltpu.make_async_copy(ref, ref, sems.at[k]).wait()

    chips = {}

    def onchip(k, start=True):
        ref = place(k, s.core)
        chips[k] = send(ref, ref, k, partner, csem, start)

    for k in (ZM0, ZM1, ZN0, ZN1):
        onchip(k, False)

    @pl.when(is1)
    def _():
        for h, k in ((0, ZM0), (1, ZM1)):
            got(k, rsem, s.core)
            for c, ch in second:
                if ch == h:
                    c.start()
            chips[k].start()

    def arrive(k):
        got(k, rsem, s.core)
        ref = place(k, s.core)
        if k == L0:
            send(ref, ref, O0, right, rsem)
        if k == R1:
            send(ref, ref, O1, left, rsem)
        for a, b, d in (
            (L0, YL0, up), (R0, YR0, up), (O0, YO0, up),
            (L1, YL1, down), (R1, YR1, down), (O1, YO1, down),
        ):
            if k == a:
                send(ref, ref, b, d, rsem)
        onchip(k)

    for k in (L0, R1, L1, R0, YL0, YR1):
        arrive(k)

    @pl.when(is1)
    def _():
        for k in (ZN0, ZN1):
            got(k, rsem, s.core)
            chips[k].start()

    for k in (O0, O1, YR0, YL1, YO0, YO1):
        arrive(k)

    for k in range(ZM0):
        got(k, csem, 1 - s.core)

    @pl.when(is0)
    def _():
        for k in (ZM0, ZM1, ZN0, ZN1):
            got(k, csem, 1 - s.core)

    conditional = {id(c) for c in zs} | {id(chips[k]) for k in (ZM0, ZM1, ZN0, ZN1)}
    for c in sent:
        if id(c) not in conditional:
            c.wait_send()

    @pl.when(is1)
    def _():
        for c in zs:
            c.wait_send()
        for k in (ZM0, ZM1, ZN0, ZN1):
            chips[k].wait_send()

    for c in owns:
        c.wait()
    swap.wait()


def gather(w_pair, tok):
    rows, cols = w_pair.shape[1:]
    hbm = pl.BlockSpec(memory_space=pl.ANY)
    return pl.pallas_call(
        gather_kernel,
        name="gather",
        out_shape=(
            jax.ShapeDtypeStruct((2, 8, rows, cols), BF),
            jax.ShapeDtypeStruct(tok.shape, BF),
        ),
        in_specs=[pl.BlockSpec(memory_space=pltpu.VMEM), hbm],
        out_specs=(hbm, hbm),
        scratch_shapes=[DMA((40,)), DMA((16,)), DMA((16,)), DMA((2,)), DMA((2,))],
        compiler_params=params(1),
    )(w_pair, tok)


def split(a):
    hi = a.astype(BF)
    return hi, (a - hi.astype(F32)).astype(BF)


def same_head():
    r = lax.broadcasted_iota(jnp.int32, (LANE, LANE), 0) // HD
    c = lax.broadcasted_iota(jnp.int32, (LANE, LANE), 1) // HD
    return r == c


def fold(block, mask):
    b = jnp.where(mask, block, 0.0)
    return b[0:32] + b[32:64] + b[64:96] + b[96:128]


def unfold(state, mask):
    return jnp.where(mask, jnp.concatenate([state] * 4, axis=0), 0.0)


def put_state(ref, state, row):
    ref[0:4] = state.reshape(4, 8, LANE)
    ref[4] = jnp.broadcast_to(row, (8, LANE))


def dot(a, b):
    return lax.dot_general(a, b, (((1,), (0,)), ((), ())), preferred_element_type=F32)


def dot_t(a, b):
    return lax.dot_general(a, b, (((0,), (0,)), ((), ())), preferred_element_type=F32)


def inside(shape, width):
    lane = lax.broadcasted_iota(jnp.int32, shape, 1) + pl.program_id(0) * LANE
    return lane < width


def project_kernel(width, tok_ref, w_ref, kv_ref, part_ref):
    both = jnp.concatenate([w_ref[0], w_ref[1]], axis=1)
    acc = dot(tok_ref[...], both)
    ok = inside((acc.shape[0], LANE), width)
    key = jnp.where(ok, jnp.maximum(acc[:, :LANE], 0.0), 0.0).astype(BF)
    val = jnp.where(ok, acc[:, LANE:], 0.0).astype(BF)
    kv_ref[0] = key
    kv_ref[1] = val
    put_state(
        part_ref,
        fold(dot_t(key, val), same_head()),
        jnp.sum(key.astype(F32), axis=0, keepdims=True),
    )


def project(tok, w):
    count, depth = tok.shape
    width = w.shape[2]
    steps = pl.cdiv(width, LANE)
    return pl.pallas_call(
        lambda *r: project_kernel(width, *r),
        name="project",
        grid=(steps,),
        out_shape=(
            jax.ShapeDtypeStruct((2, count, width), BF),
            jax.ShapeDtypeStruct((48, 8, LANE), F32),
        ),
        in_specs=[
            pl.BlockSpec((count, depth), lambda g: (0, 0)),
            pl.BlockSpec((2, depth, LANE), lambda g: (0, 0, g)),
        ],
        out_specs=(
            pl.BlockSpec((2, count, LANE), lambda g: (0, 0, g)),
            pl.BlockSpec((5, 8, LANE), lambda g: (g, 0, 0)),
        ),
        compiler_params=params(),
    )(tok, w)


def total_kernel(part_ref, out_ref, slots, ssem, rsem, ssem2, rsem2):
    s = Seat()
    me = s.sp
    peers = [(me + k) % 16 for k in range(16)]
    devs = [{"img": s.img, "sp": p} for p in peers]
    meet(devs[1:])
    out = []
    for k in range(1, 16):
        c = remote(part_ref.at[peers[k]], slots.at[k], ssem.at[k], rsem.at[k], devs[k])
        c.start()
        out.append(c)
    acc = part_ref[me]
    for k in range(1, 16):
        out[k - 1].wait_recv()
        acc = acc + slots[k]
    out_ref[me] = acc
    back = []
    for k in range(1, 16):
        c = remote(out_ref.at[me], out_ref.at[me], ssem2.at[k], rsem2.at[k], devs[k])
        c.start()
        back.append(c)
    for k in range(1, 16):
        src = (me + 16 - k) % 16
        pltpu.make_async_copy(out_ref.at[src], out_ref.at[src], rsem2.at[k]).wait()
    for c in out + back:
        c.wait_send()


def total(part, cid):
    four = part.reshape(16, 3, 8, LANE)
    vm = pl.BlockSpec(memory_space=pltpu.VMEM)
    got = pl.pallas_call(
        total_kernel,
        name=f"total{cid}",
        out_shape=jax.ShapeDtypeStruct(four.shape, F32),
        in_specs=[vm],
        out_specs=vm,
        scratch_shapes=[pltpu.VMEM(four.shape, F32)] + [DMA((16,))] * 4,
        compiler_params=params(cid),
    )(four)
    return got.reshape(48, 8, LANE)


def attend_kernel(width, q_ref, g_ref, st_ref, att_ref, dq_ref, part_ref):
    mask = same_head()
    state = st_ref[0:4].reshape(32, LANE)
    row = st_ref[4][0:1]
    kv = unfold(state, mask)
    norm = jnp.where(mask, jnp.transpose(jnp.broadcast_to(row, (LANE, LANE))), 0.0)
    kvh, kvl = split(kv)
    nh, nl = split(norm)
    kvth, kvtl = split(jnp.transpose(kv))
    ok = inside(q_ref.shape, width)
    zero = jnp.zeros((), BF)
    q = jnp.where(ok, jnp.maximum(q_ref[...], zero), zero)
    g = jnp.where(ok, g_ref[...], zero).astype(F32)
    fwd = jnp.concatenate(
        [jnp.concatenate([kvh, nh], axis=1), jnp.concatenate([kvl, nl], axis=1)], axis=0
    )
    both = dot(jnp.concatenate([q, q], axis=1), fwd)
    inv = 1.0 / (both[:, LANE:] + EPS_DEN)
    attn = both[:, :LANE] * inv
    att_ref[...] = attn.astype(BF)
    d_num = g * inv
    gah, gal = split(g * attn)
    ones = jnp.where(mask, 1.0, 0.0).astype(BF)
    dots = dot(jnp.concatenate([gah, gal], axis=1), jnp.concatenate([ones, ones], axis=0))
    d_den = -dots * inv
    pair = jnp.concatenate(split(d_num), axis=1)
    back = jnp.concatenate(
        [
            jnp.concatenate([kvth, kvtl], axis=1),
            jnp.concatenate([kvth, jnp.zeros_like(kvtl)], axis=1),
        ],
        axis=0,
    )
    feat = dot(pair, back)
    feat = feat[:, :LANE] + feat[:, LANE:] + d_den * row
    dq_ref[...] = jnp.where(q > 0, feat, 0.0).astype(BF)
    gs = dot_t(q, pair)
    put_state(
        part_ref,
        fold(gs[:, :LANE] + gs[:, LANE:], mask),
        jnp.sum(d_den * q.astype(F32), axis=0, keepdims=True),
    )


def attend(q, g, state):
    count, width = q.shape
    cols = pl.BlockSpec((count, LANE), lambda i: (0, i))
    tiles = pl.BlockSpec((5, 8, LANE), lambda i: (i, 0, 0))
    return pl.pallas_call(
        lambda *r: attend_kernel(width, *r),
        name="attend",
        grid=(pl.cdiv(width, LANE),),
        out_shape=(
            jax.ShapeDtypeStruct((count, width), BF),
            jax.ShapeDtypeStruct((count, width), BF),
            jax.ShapeDtypeStruct((48, 8, LANE), F32),
        ),
        in_specs=[cols, cols, tiles],
        out_specs=(cols, cols, tiles),
        compiler_params=params(),
    )(q, g, state)


def features_kernel(tok_img, kv_ref, st_ref, d_ref):
    mask = same_head()
    state = st_ref[0:4].reshape(32, LANE) * tok_img
    row = st_ref[4][0:1] * tok_img
    gs = unfold(state, mask)
    gh, gl = split(gs)
    th, tl = split(jnp.transpose(gs))
    key, val = kv_ref[0], kv_ref[1]
    dk = dot(jnp.concatenate([val, val], axis=1), jnp.concatenate([th, tl], axis=0)) + row
    d_ref[0] = jnp.where(key > 0, dk, 0.0).astype(BF)
    dv = dot(jnp.concatenate([key, key], axis=1), jnp.concatenate([gh, gl], axis=0))
    d_ref[1] = dv.astype(BF)


def features(kv, state, tok_img):
    _, count, width = kv.shape
    cols = pl.BlockSpec((2, count, LANE), lambda i: (0, 0, i))
    return pl.pallas_call(
        lambda *r: features_kernel(float(tok_img), *r),
        name="features",
        grid=(pl.cdiv(width, LANE),),
        out_shape=jax.ShapeDtypeStruct(kv.shape, BF),
        in_specs=[cols, pl.BlockSpec((5, 8, LANE), lambda i: (i, 0, 0))],
        out_specs=cols,
        compiler_params=params(),
    )(kv, state)


ROWS = 256


def outer_kernel(d_ref, tok, tok2, out, mine, theirs, acc, stage, ssem, rsem, lsem, osem):
    s = Seat()
    partner = s.partner()
    meet((partner,))
    swap = remote(d_ref.at[1 - s.core], theirs, ssem, rsem, partner)
    swap.start()
    load = pltpu.make_async_copy(d_ref.at[s.core], mine, lsem)
    load.start()
    load.wait()
    depth = tok.shape[1]
    whole = depth // ROWS
    rest = depth - whole * ROWS

    def one(i, _):
        at = pl.ds(pl.multiple_of(i * ROWS, ROWS), ROWS)
        acc[at] = dot_t(tok[:, at], mine[...])
        return 0

    lax.fori_loop(0, whole, one, 0)
    acc[pl.ds(whole * ROWS, rest)] = dot_t(tok[:, pl.ds(whole * ROWS, rest)], mine[...])
    swap.wait()

    def two(i, _):
        at = pl.ds(pl.multiple_of(i * ROWS, ROWS), ROWS)
        stage[at] = (acc[at] + dot_t(tok2[:, at], theirs[...])).astype(BF)
        pltpu.make_async_copy(stage.at[at], out.at[at], osem.at[i]).start()
        return 0

    lax.fori_loop(0, whole, two, 0)
    at = pl.ds(whole * ROWS, rest)
    stage[at] = (acc[at] + dot_t(tok2[:, at], theirs[...])).astype(BF)
    last = pltpu.make_async_copy(stage.at[at], out.at[at], osem.at[whole])
    last.start()
    for i in range(whole):
        at = pl.ds(i * ROWS, ROWS)
        pltpu.make_async_copy(stage.at[at], out.at[at], osem.at[i]).wait()
    last.wait()


def outer(d, tok, tok2):
    _, count, width = d.shape
    depth = tok.shape[1]
    hbm = pl.BlockSpec(memory_space=pl.ANY)
    vm = pl.BlockSpec(memory_space=pltpu.VMEM)
    return pl.pallas_call(
        outer_kernel,
        name="outer",
        out_shape=jax.ShapeDtypeStruct((depth, width), BF),
        in_specs=[hbm, vm, vm],
        out_specs=hbm,
        scratch_shapes=[
            pltpu.VMEM((count, width), BF),
            pltpu.VMEM((count, width), BF),
            pltpu.VMEM((depth, width), F32),
            pltpu.VMEM((depth, width), BF),
            DMA, DMA, DMA, DMA((depth // ROWS + 1,)),
        ],
        compiler_params=params(4),
    )(d, tok, tok2)


PIECE = 72
CUT = 640


def reduce_kernel(scale, g_ref, ok_ref, ov_ref, own, relay, final, comb, res1, relay2, final2,
                  res2, zbuf, fin, ssem, rsem, lsem, csem):
    s = Seat()
    core = s.core
    x_r, x_l, y_r, y_l = s.at(dx=1), s.at(dx=-1), s.at(dy=1), s.at(dy=-1)
    right1, left1 = s.at(dx=1 - core, dy=core), s.at(dx=core - 1, dy=-core)
    right2, left2 = s.at(dx=core, dy=1 - core), s.at(dx=-core, dy=core - 1)
    me1 = s.x * (1 - core) + s.y * core
    me2 = s.y * (1 - core) + s.x * core
    across, beside, partner = s.across(), s.beside(), s.partner()
    meet((x_r, x_l, y_r, y_l, across, beside, partner))

    def piece(h, c, j):
        xx = c * (1 - core) + j * core
        yy = j * (1 - core) + c * core
        row = pl.multiple_of(PIECE * yy - 8 * (yy // 3), 8)
        return g_ref.at[h, xx, pl.ds(row, PIECE)]

    pending = []

    def go(src, dst, i, device):
        c = remote(src, dst, ssem.at[i], rsem.at[i], device)
        c.start()
        pending.append(c)
        return c

    def go4(c, h, dst, i, device):
        for j in range(4):
            remote(piece(h, c, j), dst.at[j], ssem.at[i], rsem.at[i], device).start()
        pending.append(remote(dst, dst, ssem.at[i], rsem.at[i], device))

    def load4(c, h, dst, i):
        for j in range(4):
            pltpu.make_async_copy(piece(h, c, j), dst.at[j], lsem.at[i]).start()

    def arrived(ref, sem):
        pltpu.make_async_copy(ref, ref, sem).wait()

    def nxt(v, k):
        return (v + k) % 4

    go4(nxt(me1, 2), 0, relay.at[0], 0, right1)
    go4(nxt(me1, 2), 1, relay.at[1], 1, left1)
    go4(nxt(me1, 1), 1, final.at[0, 1], 2, right1)
    go4(nxt(me1, 3), 0, final.at[1, 0], 3, left1)
    load4(nxt(me1, 1), 0, own.at[2], 2)
    load4(nxt(me1, 3), 1, own.at[3], 3)
    load4(me1, 0, own.at[0], 0)
    load4(me1, 1, own.at[1], 1)

    def add(dst, *srcs):
        def body(j, _):
            v = srcs[0][j].astype(F32)
            for r in srcs[1:]:
                v = v + r[j].astype(F32)
            dst[j] = v.astype(BF)
            return 0

        lax.fori_loop(0, 4, body, 0)

    arrived(own.at[2], lsem.at[2])
    arrived(relay.at[0], rsem.at[0])
    add(comb.at[0], own.at[2], relay.at[0])
    go(comb.at[0], final.at[0, 0], 4, right1)
    arrived(own.at[3], lsem.at[3])
    arrived(relay.at[1], rsem.at[1])
    add(comb.at[1], own.at[3], relay.at[1])
    go(comb.at[1], final.at[1, 1], 5, left1)
    for h in range(2):
        arrived(own.at[h], lsem.at[h])
    arrived(final.at[1, 0], rsem.at[3])
    arrived(final.at[0, 1], rsem.at[2])
    arrived(final.at[0, 0], rsem.at[4])
    add(res1.at[0], own.at[0], final.at[0, 0], final.at[1, 0])

    go(res1.at[0, nxt(me2, 2)], relay2.at[0], 6, right2)
    arrived(final.at[1, 1], rsem.at[5])
    add(res1.at[1], own.at[1], final.at[0, 1], final.at[1, 1])
    go(res1.at[1, nxt(me2, 2)], relay2.at[1], 7, left2)
    go(res1.at[1, nxt(me2, 1)], final2.at[0, 1], 8, right2)
    go(res1.at[0, nxt(me2, 3)], final2.at[1, 0], 9, left2)

    def sum2(*refs):
        v = refs[0][...].astype(F32)
        for r in refs[1:]:
            v = v + r[...].astype(F32)
        return v.astype(BF)

    arrived(relay2.at[0], rsem.at[6])
    relay2[0] = sum2(relay2.at[0], res1.at[0, nxt(me2, 1)])
    go(relay2.at[0], final2.at[0, 0], 10, right2)
    arrived(relay2.at[1], rsem.at[7])
    relay2[1] = sum2(relay2.at[1], res1.at[1, nxt(me2, 3)])
    go(relay2.at[1], final2.at[1, 1], 11, left2)
    arrived(final2.at[1, 0], rsem.at[9])
    arrived(final2.at[0, 1], rsem.at[8])
    arrived(final2.at[0, 0], rsem.at[10])
    res2[0] = sum2(res1.at[0, me2], final2.at[0, 0], final2.at[1, 0])
    arrived(final2.at[1, 1], rsem.at[11])
    res2[1] = sum2(res1.at[1, me2], final2.at[0, 1], final2.at[1, 1])

    go(res2.at[1 - s.zhi], zbuf.at[0], 12, across)
    arrived(zbuf.at[0], rsem.at[12])
    zbuf[2] = sum2(res2.at[s.zhi], zbuf.at[0])
    go(zbuf.at[2], zbuf.at[1], 13, beside)
    arrived(zbuf.at[1], rsem.at[13])
    mine = fin.at[core, s.y]
    mine[...] = sum2(zbuf.at[1], zbuf.at[2])

    yd, yu, yo = (s.y + 3) % 4, (s.y + 1) % 4, (s.y + 2) % 4
    go(mine, mine, 14, y_r)
    go(mine, mine, 15, y_l)

    def chip(ref, k):
        c = remote(ref, ref, ssem.at[k], csem.at[k - 18], partner)
        c.start()
        pending.append(c)

    chip(mine, 18)
    a, b = pl.ds(0, CUT), pl.ds(CUT, mine.shape[1] - CUT)
    arrived(fin.at[core, yd], rsem.at[14])
    go(fin.at[core, yd, :, a], fin.at[core, yd, :, a], 16, y_r)
    chip(fin.at[core, yd], 19)
    arrived(fin.at[core, yu], rsem.at[15])
    go(fin.at[core, yu, :, b], fin.at[core, yu, :, b], 17, y_l)
    chip(fin.at[core, yu], 20)
    arrived(fin.at[core, yo, :, a], rsem.at[16])
    arrived(fin.at[core, yo, :, b], rsem.at[17])
    chip(fin.at[core, yo], 21)
    for k, y in enumerate((s.y, yd, yu, yo)):
        arrived(fin.at[1 - core, y], csem.at[k])
    for c in pending:
        c.wait_send()
    for ref, i in ((ok_ref, 0), (ov_ref, 1)):
        for y in range(3):
            ref[pl.ds(PIECE * y, PIECE)] = fin[i, y].astype(F32) * scale
        ref[pl.ds(216, 64)] = fin[i, 3].astype(F32)[8:] * scale


def reduce_all(g, scale):
    depth, width = g.shape
    rows = depth // 8
    vm = pl.BlockSpec(memory_space=pltpu.VMEM)
    p = (PIECE, width)
    return pl.pallas_call(
        lambda *r: reduce_kernel(scale, *r),
        name="reduce",
        out_shape=(jax.ShapeDtypeStruct((rows, width), F32),) * 2,
        in_specs=[pl.BlockSpec(memory_space=pl.ANY)],
        out_specs=(vm, vm),
        scratch_shapes=[
            pltpu.VMEM((4, 4) + p, BF),
            pltpu.VMEM((2, 4) + p, BF),
            pltpu.VMEM((2, 2, 4) + p, BF),
            pltpu.VMEM((2, 4) + p, BF),
            pltpu.VMEM((2, 4) + p, BF),
            pltpu.VMEM((2,) + p, BF),
            pltpu.VMEM((2, 2) + p, BF),
            pltpu.VMEM((2,) + p, BF),
            pltpu.VMEM((3,) + p, BF),
            pltpu.VMEM((2, 4) + p, BF),
            DMA((22,)), DMA((18,)), DMA((4,)), DMA((4,)),
        ],
        compiler_params=params(5),
    )(g.reshape(2, 4, rows, width))


def body(tokens, queries, w_key, w_value, cotangent):
    tok = tokens[0]
    count, depth = tok.shape
    width = w_key.shape[1]
    tok_img = count * lax.axis_size("sp")
    images = lax.axis_size("img")
    w4, tok2 = gather(jnp.stack([w_key, w_value]), tok)
    w = w4.reshape(2, depth, width)
    kv, part = project(tok, w)
    state = total(part, 2)
    att, dq, gpart = attend(queries[0], cotangent[0], state)
    gstate = total(gpart, 3)
    d = features(kv, gstate, tok_img)
    g = outer(d, tok, tok2)
    dwk, dwv = reduce_all(g, float((images * tok_img) ** -0.5))
    back = (((1,), (1,)), ((), ()))
    d_flat = lax.dot_general(d[0], w[0], back, preferred_element_type=F32) + lax.dot_general(
        d[1], w[1], back, preferred_element_type=F32
    )
    return att[None], d_flat.astype(BF)[None], dq[None], dwk, dwv


def solution(mesh):
    rows, flat = P("img", "sp", None), P("img", None)
    return jax.shard_map(
        body,
        mesh=mesh,
        in_specs=(rows, rows, flat, flat, rows),
        out_specs=(rows, rows, rows, flat, flat),
        check_vma=False,
    )
```

time: 612 us -> 241 us (0.39); the launches traced: 603 us -> 241 us
  blocking collectives: 285 us -> 0 us
  Pallas kernels: 0 us -> 189 us
  waiting for transfers between devices: 171 us -> 0 us
  matrix products: 80.4 us -> 15.8 us
  other arithmetic: 18 us -> 2.62 us
  between operations: 15.3 us -> 0.72 us
  starting transfers between devices: 10.2 us -> 0 us
  local copies, waits for them, and re-layouts: 22.6 us -> 32.1 us
    unnamed x1 -> x0, blocking collectives: 225 us -> none
    pallas_call x0 -> x8, Pallas kernels: none -> 189 us  [the longest x1 57.2 us: reduce_all(): pl.pallas_call(lambda *r: reduce_kernel(scale, *r), name='reduce', out_sh...]
    all_gather x2 -> x0, waiting for transfers between devices: 139 us -> none  [the longest x1 130 us: sent_together(): lax.all_gather(both, axis, axis=dim, tiled=True)]
    dot_general x13 -> x2, matrix products: 80.4 us -> 15.8 us  [the longest x1 8.11 us: body(): lax.dot_general(d[0], w[0], back, preferred_element_type=F32)]
    all_to_all x2 -> x0, blocking collectives: 59.7 us -> none  [the longest x1 36.5 us: from_everyone(): lax.all_to_all(jnp.broadcast_to(value[None], (peers, *value.shape)), axis...]
    all_to_all x1 -> x0, waiting for transfers between devices: 26.3 us -> none  [from_everyone(): lax.all_to_all(jnp.broadcast_to(value[None], (peers, *value.shape)), axis...]
    unnamed x44 -> x17, local copies, waits for them, and re-layouts: 9.33 us -> 23.4 us
    reduce_sum x3 -> x0, other arithmetic: 8.58 us -> none  [the longest x2 6.3 us: over_copies(): return from_everyone(value, axis).sum(axis=0)]
  transfers between devices with their start and end apart: 4 -> 0, of which waited for: 4 -> 0; matrix products, arithmetic and copies ran while one was open for 5% -> 0% of each run, Pallas kernels for 0% -> 0%
where the time goes in v1:
time: 241 us
  Pallas kernels  189 us (78%)
  local copies, waits for them, and re-layouts  32.1 us (13%)
  matrix products  15.8 us (7%)
  other arithmetic  2.62 us (1%)
    pallas_call x1, Pallas kernels, reduce_all(): pl.pallas_call(lambda *r: reduce_kernel(scale, *r), name='reduce', out_sh...  57.2 us
    pallas_call x1, Pallas kernels, gather(): pl.pallas_call(gather_kernel, name='gather', out_shape=(jax.ShapeDtypeStr...  45.1 us
    pallas_call x2, Pallas kernels, total(): pl.pallas_call(total_kernel, name=f'total{cid}', out_shape=jax.ShapeDtype...  29.6 us
    unnamed x17, local copies, waits for them, and re-layouts  23.4 us
    pallas_call x1, Pallas kernels, outer(): pl.pallas_call(outer_kernel, name='outer', out_shape=jax.ShapeDtypeStruct...  21.6 us
    pallas_call x1, Pallas kernels, project(): pl.pallas_call(lambda *r: project_kernel(width, *r), name='project', grid...  16.7 us
    pallas_call x1, Pallas kernels, attend(): pl.pallas_call(lambda *r: attend_kernel(width, *r), name='attend', grid=(...  10 us
    pallas_call x1, Pallas kernels, features(): pl.pallas_call(lambda *r: features_kernel(float(tok_img), *r), name='feat...  9.13 us

profile of v1, /device:TPU:1, one launch (start us, length us, event | category | flops | bytes accessed | tf_op | source)
XLA Modules:
  0.0 240.5 jit_solution(2990331207652651328)
XLA Ops:
  0.6 0.0 copy-start.2
  0.6 2.6 %pad_maximum_fusion.w_ref = bf16[2,280,1120]{2,1,0:T(8,128)(2,1)} fusion(bf16[1,280,1120]{2,1,0:T(8,128)(2,1)} %bitcast.38, bf16[1,280,1120]{2,1,0:T(8,128)(2,1)} %bitcast.39), kind=kLoop, calls=%fused_computation.5 | loop fusion | flops 627200 | bytes 2508800 | tf_op jit(solution)/shard_map/stack | solution.py:681
  3.3 4.0 %copy.10 = bf16[1,896,1120]{2,1,0:T(8,128)(2,1)} copy(bf16[1,896,1120]{1,2,0:T(8,128)(2,1)} %param.6) | data formatting | bytes 4014080 | tf_op args[1]
  7.3 0.0 copy-done.2
  7.3 2.6 %copy.11 = bf16[1,896,1120]{2,1,0:T(8,128)(2,1)} copy(bf16[1,896,1120]{1,2,0:T(8,128)(2,1)S(1)} %copy-done.2) | data formatting | bytes 4014080 | tf_op args[4]
  9.9 6.5 %copy.12 = bf16[1,896,2240]{2,1,0:T(8,128)(2,1)} copy(bf16[1,896,2240]{1,2,0:T(8,128)(2,1)} %param.5) | data formatting | bytes 8028160 | tf_op args[0]
  16.3 45.1 %gather.1 = (bf16[2,8,280,1120]{3,2,1,0:T(8,128)(2,1)}, bf16[896,2240]{1,0:T(8,128)(2,1)}) custom-call(bf16[2,280,1120]{2,1,0:T(8,128)(2,1)} %pad_maximum_fusion.w_ref, bf16[896,2240]{1,0:T(8,128)(2,1)} %bitcast.25), custom_call_target="tpu_custom_call" | custom-call | tf_op jit(solution)/shard_map/gather/pallas_call | solution.py:215
  61.5 16.7 %project.1 = (bf16[2,896,1120]{2,1,0:T(8,128)(2,1)}, f32[48,8,128]{2,1,0:T(8,128)}) custom-call(bf16[896,2240]{1,0:T(8,128)(2,1)} %bitcast.26, bf16[2,2240,1120]{2,1,0:T(8,128)(2,1)} %bitcast.28), custom_call_target="tpu_custom_call" | custom-call | tf_op jit(solution)/shard_map/project/pallas_call | solution.py:286
  78.1 15.1 %total2.1 = f32[16,3,8,128]{3,2,1,0:T(8,128)} custom-call(f32[16,3,8,128]{3,2,1,0:T(8,128)} %bitcast.41), custom_call_target="tpu_custom_call" | custom-call | tf_op jit(solution)/shard_map/total2/pallas_call | solution.py:337
  93.3 10.0 %attend.1 = (bf16[896,1120]{1,0:T(8,128)(2,1)}, bf16[896,1120]{1,0:T(8,128)(2,1)}, f32[48,8,128]{2,1,0:T(8,128)}) custom-call(bf16[896,1120]{1,0:T(8,128)(2,1)} %bitcast.30, bf16[896,1120]{1,0:T(8,128)(2,1)} %bitcast.31, f32[48,8,128]{2,1,0:T(8,128)} %bitcast.36), custom_call_target="tpu_custom_call" | custom-call | tf_op jit(solution)/shard_map/attend/pallas_call | solution.py:397
  103.3 4.1 %copy.13 = bf16[1,896,1120]{1,2,0:T(8,128)(2,1)} copy(bf16[1,896,1120]{2,1,0:T(8,128)(2,1)} %bitcast.35) | data formatting | bytes 4014080
  107.4 14.4 %total3.1 = f32[16,3,8,128]{3,2,1,0:T(8,128)} custom-call(f32[16,3,8,128]{3,2,1,0:T(8,128)} %bitcast.40), custom_call_target="tpu_custom_call" | custom-call | tf_op jit(solution)/shard_map/total3/pallas_call | solution.py:337
  121.8 9.1 %features.1.d_ref = bf16[2,896,1120]{2,1,0:T(8,128)(2,1)} custom-call(bf16[2,896,1120]{2,1,0:T(8,128)(2,1)} %get-tuple-element.17.r_0_, f32[48,8,128]{2,1,0:T(8,128)} %bitcast.37), custom_call_target="tpu_custom_call" | custom-call | tf_op jit(solution)/shard_map/features/pallas_call | solution.py:429
  130.9 21.6 %outer.1 = bf16[2240,1120]{1,0:T(8,128)(2,1)} custom-call(bf16[2,896,1120]{2,1,0:T(8,128)(2,1)} %features.1.d_ref, bf16[896,2240]{1,0:T(8,128)(2,1)} %bitcast.27, bf16[896,2240]{1,0:T(8,128)(2,1)} %get-tuple-element.20.tok2), custom_call_target="tpu_custom_call" | custom-call | tf_op jit(solution)/shard_map/outer/pallas_call | solution.py:487
  152.6 57.2 %reduce.1 = (f32[280,1120]{1,0:T(8,128)}, f32[280,1120]{1,0:T(8,128)}) custom-call(bf16[2,4,280,1120]{3,2,1,0:T(8,128)(2,1)} %bitcast.29), custom_call_target="tpu_custom_call" | custom-call | tf_op jit(solution)/shard_map/reduce/pallas_call | solution.py:652
  209.8 4.1 %copy.14 = bf16[1,896,1120]{1,2,0:T(8,128)(2,1)} copy(bf16[1,896,1120]{2,1,0:T(8,128)(2,1)} %bitcast.34) | data formatting | bytes 4014080
  213.9 0.0 copy-start
  213.9 8.7 %fusion.2 = (bf16[1,8,280,1120]{3,2,1,0:T(8,128)(2,1)}, bf16[1,8,280,1120]{3,2,1,0:T(8,128)(2,1)}) fusion(bf16[2,8,280,1120]{3,2,1,0:T(8,128)(2,1)} %get-tuple-element.14), kind=kLoop, calls=%fused_computation.6 | loop fusion | bytes 20070400 | tf_op jit(solution)/shard_map/slice | solution.py:692
  222.6 0.0 copy-done
  222.6 0.0 copy-start.1
  222.6 8.1 %fusion.1 = f32[896,2240]{0,1:T(8,128)S(1)} fusion(bf16[2240,1120]{1,0:T(8,128)(2,1)} %bitcast.33, bf16[2,896,1120]{2,1,0:T(8,128)(2,1)S(1)} %copy-done), kind=kOutput, calls=%fused_computation.4 | convolution fusion | flops 4495769600 | bytes 15110144 | tf_op jit(solution)/shard_map/dot_general | solution.py:691
  230.7 0.0 copy-done.1
  230.7 0.0 copy-start.4
  230.7 0.0 copy-start.3
  230.7 7.7 %fusion = bf16[1,896,2240]{1,2,0:T(8,128)(2,1)} fusion(f32[896,2240]{0,1:T(8,128)S(1)} %fusion.1, bf16[2240,1120]{1,0:T(8,128)(2,1)S(1)} %bitcast.32, bf16[2,896,1120]{2,1,0:T(8,128)(2,1)S(1)} %copy-done), kind=kOutput, calls=%fused_computation.1 | convolution fusion | flops 4499783680 | bytes 19267584 | tf_op jit(solution)/shard_map/dot_general | solution.py:691
  238.4 0.0 copy-done.4
  238.4 1.0 copy.17
  239.5 0.0 copy-done.3
  239.5 1.0 copy.18
Async XLA Ops:
  0.6 6.7 %copy-start.2 = (bf16[1,896,1120]{1,2,0:T(8,128)(2,1)S(1)}, bf16[1,896,1120]{1,2,0:T(8,128)(2,1)}, u32[]{:S(2)}) copy-start(bf16[1,896,1120]{1,2,0:T(8,128)(2,1)} %param.9) | copy-start | bytes 6021124
  213.9 8.7 %copy-start = (bf16[2,896,1120]{2,1,0:T(8,128)(2,1)S(1)}, bf16[2,896,1120]{2,1,0:T(8,128)(2,1)}, u32[]{:S(2)}) copy-start(bf16[2,896,1120]{2,1,0:T(8,128)(2,1)} %features.1.d_ref) | copy-start | bytes 12042244
  222.6 8.1 %copy-start.1 = (bf16[1,8,280,1120]{3,2,1,0:T(8,128)(2,1)S(1)}, bf16[1,8,280,1120]{3,2,1,0:T(8,128)(2,1)}, u32[]{:S(2)}) copy-start(bf16[1,8,280,1120]{3,2,1,0:T(8,128)(2,1)} %get-tuple-element.28) | copy-start | bytes 15052804
  230.7 7.7 %copy-start.4 = (f32[280,1120]{1,0:T(8,128)S(1)}, f32[280,1120]{1,0:T(8,128)}, u32[]{:S(2)}) copy-start(f32[280,1120]{1,0:T(8,128)} %get-tuple-element.38) | copy-start | bytes 3763204
  230.7 8.7 %copy-start.3 = (f32[280,1120]{1,0:T(8,128)S(1)}, f32[280,1120]{1,0:T(8,128)}, u32[]{:S(2)}) copy-start(f32[280,1120]{1,0:T(8,128)} %get-tuple-element.39) | copy-start | bytes 3763204

commit v2 on v1

--- a/solution.py
+++ b/solution.py
@@ -11,6 +11,7 @@
 F32 = jnp.float32
 MESH = pl.DeviceIdType.MESH
 LANE = 128
+ROWS = 256
 VMEM_MAX = 64 * 1024 * 1024 - 65536
 DMA = pltpu.SemaphoreType.DMA
 
@@ -66,13 +67,23 @@
 L0, L1, R0, R1, O0, O1, YL0, YR0, YO0, YL1, YR1, YO1, ZM0, ZM1, ZN0, ZN1 = range(16)
 
 
-def gather_kernel(w_ref, tok_ref, out, tok_out, ssem, rsem, csem, lsem, tsem):
+def gather_kernel(wk_ref, wv_ref, tok_ref, out, tok_out, tok_t, w_ref, tin, tup, ssem, rsem, csem,
+                  lsem, tsem, usem):
     s = Seat()
     m = s.y % 2
     right, left = s.at(dx=1), s.at(dx=-1)
     up, down = s.at(dy=1), s.at(dy=-1)
     partner, across = s.partner(), s.across()
+    loads = [
+        pltpu.make_async_copy(r, w_ref.at[i], lsem.at[2 + i]) for i, r in enumerate((wk_ref, wv_ref))
+    ]
+    read = pltpu.make_async_copy(tok_ref, tin, usem.at[0])
+    for c in loads:
+        c.start()
+    read.start()
     meet((right, left, up, down, partner, across))
+    for c in loads:
+        c.wait()
 
     def part(mat, shard, h):
         return out.at[mat, shard, pl.ds(HALVES[h][0], HALVES[h][1])]
@@ -134,6 +145,21 @@
     for c in owns:
         c.start()
     swap.start()
+    read.wait()
+    depth = tok_ref.shape[0]
+    whole = depth // ROWS
+    rest = depth - whole * ROWS
+
+    def flip(i, _):
+        at = pl.ds(pl.multiple_of(i * ROWS, ROWS), ROWS)
+        tup[:, at] = jnp.transpose(tin[at])
+        return 0
+
+    lax.fori_loop(0, whole, flip, 0)
+    at = pl.ds(whole * ROWS, rest)
+    tup[:, at] = jnp.transpose(tin[at])
+    write = pltpu.make_async_copy(tup, tok_t, usem.at[1])
+    write.start()
 
     def got(k, sems, core):
         ref = place(k, core)
@@ -207,10 +233,11 @@
     for c in owns:
         c.wait()
     swap.wait()
-
-
-def gather(w_pair, tok):
-    rows, cols = w_pair.shape[1:]
+    write.wait()
+
+
+def gather(wk, wv, tok):
+    rows, cols = wk.shape
     hbm = pl.BlockSpec(memory_space=pl.ANY)
     return pl.pallas_call(
         gather_kernel,
@@ -218,12 +245,18 @@
         out_shape=(
             jax.ShapeDtypeStruct((2, 8, rows, cols), BF),
             jax.ShapeDtypeStruct(tok.shape, BF),
+            jax.ShapeDtypeStruct(tok.shape[::-1], BF),
         ),
-        in_specs=[pl.BlockSpec(memory_space=pltpu.VMEM), hbm],
-        out_specs=(hbm, hbm),
-        scratch_shapes=[DMA((40,)), DMA((16,)), DMA((16,)), DMA((2,)), DMA((2,))],
+        in_specs=[hbm] * 3,
+        out_specs=(hbm,) * 3,
+        scratch_shapes=[
+            pltpu.VMEM((2, rows, cols), BF),
+            pltpu.VMEM(tok.shape, BF),
+            pltpu.VMEM(tok.shape[::-1], BF),
+            DMA((40,)), DMA((16,)), DMA((16,)), DMA((4,)), DMA((2,)), DMA((2,)),
+        ],
         compiler_params=params(1),
-    )(w_pair, tok)
+    )(wk, wv, tok)
 
 
 def split(a):
@@ -346,65 +379,65 @@
     return got.reshape(48, 8, LANE)
 
 
+def dot_r(a, b):
+    return lax.dot_general(a, b, (((1,), (1,)), ((), ())), preferred_element_type=F32)
+
+
 def attend_kernel(width, q_ref, g_ref, st_ref, att_ref, dq_ref, part_ref):
     mask = same_head()
     state = st_ref[0:4].reshape(32, LANE)
-    row = st_ref[4][0:1]
+    row = jnp.broadcast_to(st_ref[4][0:1], (LANE, LANE))
+    col = jnp.transpose(row)[:, 0:1]
     kv = unfold(state, mask)
-    norm = jnp.where(mask, jnp.transpose(jnp.broadcast_to(row, (LANE, LANE))), 0.0)
     kvh, kvl = split(kv)
-    nh, nl = split(norm)
     kvth, kvtl = split(jnp.transpose(kv))
-    ok = inside(q_ref.shape, width)
+    nh, nl = split(jnp.where(mask, row, 0.0))
+    line = lax.broadcasted_iota(jnp.int32, q_ref.shape, 0) + pl.program_id(0) * LANE
+    ok = line < width
     zero = jnp.zeros((), BF)
     q = jnp.where(ok, jnp.maximum(q_ref[...], zero), zero)
     g = jnp.where(ok, g_ref[...], zero).astype(F32)
     fwd = jnp.concatenate(
-        [jnp.concatenate([kvh, nh], axis=1), jnp.concatenate([kvl, nl], axis=1)], axis=0
+        [jnp.concatenate([kvth, kvtl], axis=1), jnp.concatenate([nh, nl], axis=1)], axis=0
     )
-    both = dot(jnp.concatenate([q, q], axis=1), fwd)
-    inv = 1.0 / (both[:, LANE:] + EPS_DEN)
-    attn = both[:, :LANE] * inv
+    both = dot(fwd, jnp.concatenate([q, q], axis=0))
+    inv = 1.0 / (both[LANE:] + EPS_DEN)
+    attn = both[:LANE] * inv
     att_ref[...] = attn.astype(BF)
     d_num = g * inv
-    gah, gal = split(g * attn)
     ones = jnp.where(mask, 1.0, 0.0).astype(BF)
-    dots = dot(jnp.concatenate([gah, gal], axis=1), jnp.concatenate([ones, ones], axis=0))
+    dots = dot(
+        jnp.concatenate([ones, ones], axis=1), jnp.concatenate(split(g * attn), axis=0)
+    )
     d_den = -dots * inv
-    pair = jnp.concatenate(split(d_num), axis=1)
-    back = jnp.concatenate(
-        [
-            jnp.concatenate([kvth, kvtl], axis=1),
-            jnp.concatenate([kvth, jnp.zeros_like(kvtl)], axis=1),
-        ],
-        axis=0,
-    )
-    feat = dot(pair, back)
-    feat = feat[:, :LANE] + feat[:, LANE:] + d_den * row
+    dnh, dnl = split(d_num)
+    feat = dot(jnp.concatenate([kvh, kvh], axis=1), jnp.concatenate([dnh, dnl], axis=0))
+    feat = feat + dot(kvl, dnh) + d_den * col
     dq_ref[...] = jnp.where(q > 0, feat, 0.0).astype(BF)
-    gs = dot_t(q, pair)
+    gs = dot_r(q, jnp.concatenate([dnh, dnl], axis=0))
+    gn = jnp.sum(d_den * q.astype(F32), axis=1, keepdims=True)
     put_state(
         part_ref,
         fold(gs[:, :LANE] + gs[:, LANE:], mask),
-        jnp.sum(d_den * q.astype(F32), axis=0, keepdims=True),
+        jnp.transpose(jnp.broadcast_to(gn, (LANE, LANE)))[0:1],
     )
 
 
 def attend(q, g, state):
-    count, width = q.shape
-    cols = pl.BlockSpec((count, LANE), lambda i: (0, i))
+    width, count = q.shape
+    lines = pl.BlockSpec((LANE, count), lambda i: (i, 0))
     tiles = pl.BlockSpec((5, 8, LANE), lambda i: (i, 0, 0))
     return pl.pallas_call(
         lambda *r: attend_kernel(width, *r),
         name="attend",
         grid=(pl.cdiv(width, LANE),),
         out_shape=(
-            jax.ShapeDtypeStruct((count, width), BF),
-            jax.ShapeDtypeStruct((count, width), BF),
+            jax.ShapeDtypeStruct((width, count), BF),
+            jax.ShapeDtypeStruct((width, count), BF),
             jax.ShapeDtypeStruct((48, 8, LANE), F32),
         ),
-        in_specs=[cols, cols, tiles],
-        out_specs=(cols, cols, tiles),
+        in_specs=[lines, lines, tiles],
+        out_specs=(lines, lines, tiles),
         compiler_params=params(),
     )(q, g, state)
 
@@ -437,76 +470,15 @@
     )(kv, state)
 
 
-ROWS = 256
-
-
-def outer_kernel(d_ref, tok, tok2, out, mine, theirs, acc, stage, ssem, rsem, lsem, osem):
-    s = Seat()
-    partner = s.partner()
-    meet((partner,))
-    swap = remote(d_ref.at[1 - s.core], theirs, ssem, rsem, partner)
-    swap.start()
-    load = pltpu.make_async_copy(d_ref.at[s.core], mine, lsem)
-    load.start()
-    load.wait()
-    depth = tok.shape[1]
-    whole = depth // ROWS
-    rest = depth - whole * ROWS
-
-    def one(i, _):
-        at = pl.ds(pl.multiple_of(i * ROWS, ROWS), ROWS)
-        acc[at] = dot_t(tok[:, at], mine[...])
-        return 0
-
-    lax.fori_loop(0, whole, one, 0)
-    acc[pl.ds(whole * ROWS, rest)] = dot_t(tok[:, pl.ds(whole * ROWS, rest)], mine[...])
-    swap.wait()
-
-    def two(i, _):
-        at = pl.ds(pl.multiple_of(i * ROWS, ROWS), ROWS)
-        stage[at] = (acc[at] + dot_t(tok2[:, at], theirs[...])).astype(BF)
-        pltpu.make_async_copy(stage.at[at], out.at[at], osem.at[i]).start()
-        return 0
-
-    lax.fori_loop(0, whole, two, 0)
-    at = pl.ds(whole * ROWS, rest)
-    stage[at] = (acc[at] + dot_t(tok2[:, at], theirs[...])).astype(BF)
-    last = pltpu.make_async_copy(stage.at[at], out.at[at], osem.at[whole])
-    last.start()
-    for i in range(whole):
-        at = pl.ds(i * ROWS, ROWS)
-        pltpu.make_async_copy(stage.at[at], out.at[at], osem.at[i]).wait()
-    last.wait()
-
-
-def outer(d, tok, tok2):
-    _, count, width = d.shape
-    depth = tok.shape[1]
-    hbm = pl.BlockSpec(memory_space=pl.ANY)
-    vm = pl.BlockSpec(memory_space=pltpu.VMEM)
-    return pl.pallas_call(
-        outer_kernel,
-        name="outer",
-        out_shape=jax.ShapeDtypeStruct((depth, width), BF),
-        in_specs=[hbm, vm, vm],
-        out_specs=hbm,
-        scratch_shapes=[
-            pltpu.VMEM((count, width), BF),
-            pltpu.VMEM((count, width), BF),
-            pltpu.VMEM((depth, width), F32),
-            pltpu.VMEM((depth, width), BF),
-            DMA, DMA, DMA, DMA((depth // ROWS + 1,)),
-        ],
-        compiler_params=params(4),
-    )(d, tok, tok2)
-
-
 PIECE = 72
+OFFS = (0, 72, 144, 208)
 CUT = 640
-
-
-def reduce_kernel(scale, g_ref, ok_ref, ov_ref, own, relay, final, comb, res1, relay2, final2,
-                  res2, zbuf, fin, ssem, rsem, lsem, csem):
+BAND = 448
+
+
+def finish_kernel(scale, d_ref, tok_ref, tok2_ref, w_ref, ok_ref, ov_ref, dt_ref, cat, dcat, dboth,
+                  gp, relay, final, comb, res1, relay2, final2, res2, zbuf, fin, wbuf, tbuf,
+                  ssem, rsem, lsem, csem, wsem, osem):
     s = Seat()
     core = s.core
     x_r, x_l, y_r, y_l = s.at(dx=1), s.at(dx=-1), s.at(dy=1), s.at(dy=-1)
@@ -515,30 +487,41 @@
     me1 = s.x * (1 - core) + s.y * core
     me2 = s.y * (1 - core) + s.x * core
     across, beside, partner = s.across(), s.beside(), s.partner()
+    count = d_ref.shape[1]
+
+    def loader(src, dst, i):
+        return pltpu.make_async_copy(src, dst, lsem.at[i])
+
+    lo, up = pl.ds(0, count), pl.ds(count, count)
+    ld = [
+        loader(d_ref.at[core], dcat.at[lo], 0),
+        loader(tok_ref, cat.at[:, :, lo], 1),
+        loader(tok2_ref, cat.at[:, :, up], 2),
+        loader(d_ref, dboth, 3),
+    ]
+    for c in ld:
+        c.start()
+    bands = w_ref.shape[1] // BAND
+
+    def band_load(i):
+        at = pl.ds(i * BAND, BAND)
+        return pltpu.make_async_copy(w_ref.at[:, at], wbuf.at[i % 2], wsem.at[i])
+
+    band_load(0).start()
+    band_load(1).start()
     meet((x_r, x_l, y_r, y_l, across, beside, partner))
-
-    def piece(h, c, j):
-        xx = c * (1 - core) + j * core
-        yy = j * (1 - core) + c * core
-        row = pl.multiple_of(PIECE * yy - 8 * (yy // 3), 8)
-        return g_ref.at[h, xx, pl.ds(row, PIECE)]
+    swap = remote(d_ref.at[1 - core], dcat.at[up], ssem.at[22], rsem.at[18], partner)
+    swap.start()
 
     pending = []
 
+    def copy(src, dst, i, device):
+        return remote(src, dst, ssem.at[i], rsem.at[i], device)
+
     def go(src, dst, i, device):
-        c = remote(src, dst, ssem.at[i], rsem.at[i], device)
+        c = copy(src, dst, i, device)
         c.start()
         pending.append(c)
-        return c
-
-    def go4(c, h, dst, i, device):
-        for j in range(4):
-            remote(piece(h, c, j), dst.at[j], ssem.at[i], rsem.at[i], device).start()
-        pending.append(remote(dst, dst, ssem.at[i], rsem.at[i], device))
-
-    def load4(c, h, dst, i):
-        for j in range(4):
-            pltpu.make_async_copy(piece(h, c, j), dst.at[j], lsem.at[i]).start()
 
     def arrived(ref, sem):
         pltpu.make_async_copy(ref, ref, sem).wait()
@@ -546,14 +529,53 @@
     def nxt(v, k):
         return (v + k) % 4
 
-    go4(nxt(me1, 2), 0, relay.at[0], 0, right1)
-    go4(nxt(me1, 2), 1, relay.at[1], 1, left1)
-    go4(nxt(me1, 1), 1, final.at[0, 1], 2, right1)
-    go4(nxt(me1, 3), 0, final.at[1, 0], 3, left1)
-    load4(nxt(me1, 1), 0, own.at[2], 2)
-    load4(nxt(me1, 3), 1, own.at[3], 3)
-    load4(me1, 0, own.at[0], 0)
-    load4(me1, 1, own.at[1], 1)
+    def bands_out(i):
+        at = pl.ds(i * BAND, BAND)
+        return pltpu.make_async_copy(tbuf.at[i % 2], dt_ref.at[at], osem.at[i])
+
+    def band(i):
+        if i == 0:
+            ld[3].wait()
+        band_load(i).wait()
+        if i >= 2:
+            bands_out(i - 2).wait()
+        both = wbuf.at[i % 2]
+        v = dot_r(both[0], dboth[0]) + dot_r(both[1], dboth[1])
+        tbuf[i % 2] = v.astype(BF)
+        bands_out(i).start()
+        if i + 2 < bands:
+            band_load(i + 2).start()
+
+    def shard(h, dx):
+        xx = nxt(s.x, dx)
+        v = dot(cat[h * 4 + xx], dcat[...])
+        for y in range(4):
+            c = xx * (1 - core) + y * core
+            j = y * (1 - core) + xx * core
+            gp[h, c, j] = v[OFFS[y] : OFFS[y] + PIECE].astype(BF)
+
+        @pl.when(core == 1)
+        def _():
+            j = xx
+            d = (right1, left1)
+            copy(gp.at[h, nxt(me1, 2), j], relay.at[h, j], h, d[h]).start()
+            if h == 1:
+                copy(gp.at[1, nxt(me1, 1), j], final.at[0, 1, j], 2, right1).start()
+            else:
+                copy(gp.at[0, nxt(me1, 3), j], final.at[1, 0, j], 3, left1).start()
+
+        act = {
+            (0, 2): (relay.at[0], 0, right1),
+            (1, 2): (relay.at[1], 1, left1),
+            (1, 1): (final.at[0, 1], 2, right1),
+            (0, 3): (final.at[1, 0], 3, left1),
+        }.get((h, dx))
+        if act is not None:
+            dst, i, dev = act
+
+            @pl.when(core == 0)
+            def _():
+                copy(gp.at[h, nxt(me1, dx)], dst, i, dev).start()
 
     def add(dst, *srcs):
         def body(j, _):
@@ -565,54 +587,79 @@
 
         lax.fori_loop(0, 4, body, 0)
 
-    arrived(own.at[2], lsem.at[2])
-    arrived(relay.at[0], rsem.at[0])
-    add(comb.at[0], own.at[2], relay.at[0])
-    go(comb.at[0], final.at[0, 0], 4, right1)
-    arrived(own.at[3], lsem.at[3])
-    arrived(relay.at[1], rsem.at[1])
-    add(comb.at[1], own.at[3], relay.at[1])
-    go(comb.at[1], final.at[1, 1], 5, left1)
-    for h in range(2):
-        arrived(own.at[h], lsem.at[h])
+    def combine():
+        arrived(relay.at[0], rsem.at[0])
+        add(comb.at[0], gp.at[0, nxt(me1, 1)], relay.at[0])
+        copy(comb.at[0], final.at[0, 0], 4, right1).start()
+        arrived(relay.at[1], rsem.at[1])
+        add(comb.at[1], gp.at[1, nxt(me1, 3)], relay.at[1])
+        copy(comb.at[1], final.at[1, 1], 5, left1).start()
+
+    for c in ld[:3]:
+        c.wait()
+    swap.wait()
+    for h, dx in ((0, 2), (1, 2), (1, 1), (0, 3), (0, 1), (1, 3)):
+        shard(h, dx)
+
+    @pl.when(core == 0)
+    def _():
+        combine()
+
+    shard(0, 0)
+    shard(1, 0)
+
+    @pl.when(core == 1)
+    def _():
+        combine()
+
+    for i, dst in enumerate(
+        (relay.at[0], relay.at[1], final.at[0, 1], final.at[1, 0], final.at[0, 0], final.at[1, 1])
+    ):
+        pending.append(copy(dst, dst, i, right1))
+
+    band(0)
+    band(1)
+    band(2)
     arrived(final.at[1, 0], rsem.at[3])
     arrived(final.at[0, 1], rsem.at[2])
     arrived(final.at[0, 0], rsem.at[4])
-    add(res1.at[0], own.at[0], final.at[0, 0], final.at[1, 0])
+    add(res1.at[0], gp.at[0, me1], final.at[0, 0], final.at[1, 0])
 
     go(res1.at[0, nxt(me2, 2)], relay2.at[0], 6, right2)
     arrived(final.at[1, 1], rsem.at[5])
-    add(res1.at[1], own.at[1], final.at[0, 1], final.at[1, 1])
+    add(res1.at[1], gp.at[1, me1], final.at[0, 1], final.at[1, 1])
     go(res1.at[1, nxt(me2, 2)], relay2.at[1], 7, left2)
     go(res1.at[1, nxt(me2, 1)], final2.at[0, 1], 8, right2)
     go(res1.at[0, nxt(me2, 3)], final2.at[1, 0], 9, left2)
-
-    def sum2(*refs):
+    band(3)
+
+    def plus(*refs):
         v = refs[0][...].astype(F32)
         for r in refs[1:]:
             v = v + r[...].astype(F32)
         return v.astype(BF)
 
     arrived(relay2.at[0], rsem.at[6])
-    relay2[0] = sum2(relay2.at[0], res1.at[0, nxt(me2, 1)])
+    relay2[0] = plus(relay2.at[0], res1.at[0, nxt(me2, 1)])
     go(relay2.at[0], final2.at[0, 0], 10, right2)
     arrived(relay2.at[1], rsem.at[7])
-    relay2[1] = sum2(relay2.at[1], res1.at[1, nxt(me2, 3)])
+    relay2[1] = plus(relay2.at[1], res1.at[1, nxt(me2, 3)])
     go(relay2.at[1], final2.at[1, 1], 11, left2)
+    band(4)
     arrived(final2.at[1, 0], rsem.at[9])
     arrived(final2.at[0, 1], rsem.at[8])
     arrived(final2.at[0, 0], rsem.at[10])
-    res2[0] = sum2(res1.at[0, me2], final2.at[0, 0], final2.at[1, 0])
+    res2[0] = plus(res1.at[0, me2], final2.at[0, 0], final2.at[1, 0])
     arrived(final2.at[1, 1], rsem.at[11])
-    res2[1] = sum2(res1.at[1, me2], final2.at[0, 1], final2.at[1, 1])
+    res2[1] = plus(res1.at[1, me2], final2.at[0, 1], final2.at[1, 1])
 
     go(res2.at[1 - s.zhi], zbuf.at[0], 12, across)
     arrived(zbuf.at[0], rsem.at[12])
-    zbuf[2] = sum2(res2.at[s.zhi], zbuf.at[0])
+    zbuf[2] = plus(res2.at[s.zhi], zbuf.at[0])
     go(zbuf.at[2], zbuf.at[1], 13, beside)
     arrived(zbuf.at[1], rsem.at[13])
     mine = fin.at[core, s.y]
-    mine[...] = sum2(zbuf.at[1], zbuf.at[2])
+    mine[...] = plus(zbuf.at[1], zbuf.at[2])
 
     yd, yu, yo = (s.y + 3) % 4, (s.y + 1) % 4, (s.y + 2) % 4
     go(mine, mine, 14, y_r)
@@ -638,25 +685,33 @@
         arrived(fin.at[1 - core, y], csem.at[k])
     for c in pending:
         c.wait_send()
+    for i in (bands - 2, bands - 1):
+        bands_out(i).wait()
     for ref, i in ((ok_ref, 0), (ov_ref, 1)):
         for y in range(3):
             ref[pl.ds(PIECE * y, PIECE)] = fin[i, y].astype(F32) * scale
         ref[pl.ds(216, 64)] = fin[i, 3].astype(F32)[8:] * scale
 
 
-def reduce_all(g, scale):
-    depth, width = g.shape
+def finish(d, tok, tok2, w, scale):
+    _, count, width = d.shape
+    depth = tok.shape[0]
     rows = depth // 8
     vm = pl.BlockSpec(memory_space=pltpu.VMEM)
+    hbm = pl.BlockSpec(memory_space=pl.ANY)
     p = (PIECE, width)
     return pl.pallas_call(
-        lambda *r: reduce_kernel(scale, *r),
-        name="reduce",
-        out_shape=(jax.ShapeDtypeStruct((rows, width), F32),) * 2,
-        in_specs=[pl.BlockSpec(memory_space=pl.ANY)],
-        out_specs=(vm, vm),
+        lambda *r: finish_kernel(scale, *r),
+        name="finish",
+        out_shape=(jax.ShapeDtypeStruct((rows, width), F32),) * 2
+        + (jax.ShapeDtypeStruct((depth, count), BF),),
+        in_specs=[hbm] * 4,
+        out_specs=(vm, vm, hbm),
         scratch_shapes=[
-            pltpu.VMEM((4, 4) + p, BF),
+            pltpu.VMEM((8, rows, 2 * count), BF),
+            pltpu.VMEM((2 * count, width), BF),
+            pltpu.VMEM((2, count, width), BF),
+            pltpu.VMEM((2, 4, 4) + p, BF),
             pltpu.VMEM((2, 4) + p, BF),
             pltpu.VMEM((2, 2, 4) + p, BF),
             pltpu.VMEM((2, 4) + p, BF),
@@ -666,32 +721,29 @@
             pltpu.VMEM((2,) + p, BF),
             pltpu.VMEM((3,) + p, BF),
             pltpu.VMEM((2, 4) + p, BF),
-            DMA((22,)), DMA((18,)), DMA((4,)), DMA((4,)),
+            pltpu.VMEM((2, 2, BAND, width), BF),
+            pltpu.VMEM((2, BAND, count), BF),
+            DMA((23,)), DMA((19,)), DMA((4,)), DMA((4,)), DMA((5,)), DMA((5,)),
         ],
         compiler_params=params(5),
-    )(g.reshape(2, 4, rows, width))
+    )(d, tok.reshape(8, rows, count), tok2.reshape(8, rows, count), w)
 
 
 def body(tokens, queries, w_key, w_value, cotangent):
-    tok = tokens[0]
-    count, depth = tok.shape
+    tok = jnp.transpose(tokens[0])
+    depth, count = tok.shape
     width = w_key.shape[1]
     tok_img = count * lax.axis_size("sp")
     images = lax.axis_size("img")
-    w4, tok2 = gather(jnp.stack([w_key, w_value]), tok)
+    w4, tok2, tok_t = gather(w_key, w_value, tok)
     w = w4.reshape(2, depth, width)
-    kv, part = project(tok, w)
+    kv, part = project(tok_t, w)
     state = total(part, 2)
-    att, dq, gpart = attend(queries[0], cotangent[0], state)
+    att, dq, gpart = attend(jnp.transpose(queries[0]), jnp.transpose(cotangent[0]), state)
     gstate = total(gpart, 3)
     d = features(kv, gstate, tok_img)
-    g = outer(d, tok, tok2)
-    dwk, dwv = reduce_all(g, float((images * tok_img) ** -0.5))
-    back = (((1,), (1,)), ((), ()))
-    d_flat = lax.dot_general(d[0], w[0], back, preferred_element_type=F32) + lax.dot_general(
-        d[1], w[1], back, preferred_element_type=F32
-    )
-    return att[None], d_flat.astype(BF)[None], dq[None], dwk, dwv
+    dwk, dwv, dt = finish(d, tok, tok2, w, float((images * tok_img) ** -0.5))
+    return jnp.transpose(att)[None], jnp.transpose(dt)[None], jnp.transpose(dq)[None], dwk, dwv
 
 
 def solution(mesh):

time: 241 us -> 184 us (0.76)
  local copies, waits for them, and re-layouts: 32.1 us -> 6.66 us
  matrix products: 15.8 us -> 0 us
  Pallas kernels: 189 us -> 176 us
  other arithmetic: 2.62 us -> 0 us
    unnamed x17 -> x7, local copies, waits for them, and re-layouts: 23.4 us -> 6.66 us
    dot_general x2 -> x0, matrix products: 15.8 us -> none  [the longest x1 8.11 us: body(): lax.dot_general(d[0], w[0], back, preferred_element_type=F32)]
    pallas_call x2 -> x1, Pallas kernels: 78.8 us -> 64.9 us  [finish(): pl.pallas_call(lambda *r: finish_kernel(scale, *r), name='finish', out_sh...]
    slice x1 -> x0, local copies, waits for them, and re-layouts: 8.74 us -> none  [body(): w[1]]
    another operation x1 -> x0, other arithmetic: 2.62 us -> none  [body(): w4, tok2 = gather(jnp.stack([w_key, w_value]), tok)]
where the time goes in v2:
time: 184 us; the launch traced here: 183 us
  Pallas kernels  176 us (96%)
  local copies, waits for them, and re-layouts  6.66 us (4%)
    pallas_call x1, Pallas kernels, finish(): pl.pallas_call(lambda *r: finish_kernel(scale, *r), name='finish', out_sh...  64.9 us
    pallas_call x1, Pallas kernels, gather(): pl.pallas_call(gather_kernel, name='gather', out_shape=(jax.ShapeDtypeStr...  43.7 us
    pallas_call x2, Pallas kernels, total(): pl.pallas_call(total_kernel, name=f'total{cid}', out_shape=jax.ShapeDtype...  29.7 us
    pallas_call x1, Pallas kernels, project(): pl.pallas_call(lambda *r: project_kernel(width, *r), name='project', grid...  16.7 us
    pallas_call x1, Pallas kernels, attend(): pl.pallas_call(lambda *r: attend_kernel(width, *r), name='attend', grid=(...  11.9 us
    pallas_call x1, Pallas kernels, features(): pl.pallas_call(lambda *r: features_kernel(float(tok_img), *r), name='feat...  9.12 us
    unnamed x7, local copies, waits for them, and re-layouts  6.66 us

profile of v2, /device:TPU:1, one launch (start us, length us, event | category | flops | bytes accessed | tf_op | source)
XLA Modules:
  0.0 183.3 jit_solution(1321526931221369720)
XLA Ops:
  0.6 43.7 %gather.1 = (bf16[2,8,280,1120]{3,2,1,0:T(8,128)(2,1)}, bf16[2240,896]{1,0:T(8,128)(2,1)}, bf16[896,2240]{1,0:T(8,128)(2,1)}) custom-call(bf16[280,1120]{1,0:T(8,128)(2,1)} %wk_ref.1, bf16[280,1120]{1,0:T(8,128)(2,1)} %wv_ref.1, bf16[2240,896]{1,0:T(8,128)(2,1)} %bitcast.28), custom_call_target="tpu_custom_call" | custom-call | tf_op jit(solution)/shard_map/gather/pallas_call | solution.py:242
  44.4 16.7 %project.1 = (bf16[2,896,1120]{2,1,0:T(8,128)(2,1)}, f32[48,8,128]{2,1,0:T(8,128)}) custom-call(bf16[896,2240]{1,0:T(8,128)(2,1)} %get-tuple-element.16.r_0_, bf16[2,2240,1120]{2,1,0:T(8,128)(2,1)} %bitcast.26), custom_call_target="tpu_custom_call" | custom-call | tf_op jit(solution)/shard_map/project/pallas_call | solution.py:319
  61.0 15.3 %total2.1 = f32[16,3,8,128]{3,2,1,0:T(8,128)} custom-call(f32[16,3,8,128]{3,2,1,0:T(8,128)} %bitcast.37), custom_call_target="tpu_custom_call" | custom-call | tf_op jit(solution)/shard_map/total2/pallas_call | solution.py:370
  76.3 11.9 %attend.1 = (bf16[1120,896]{1,0:T(8,128)(2,1)}, bf16[1120,896]{1,0:T(8,128)(2,1)}, f32[48,8,128]{2,1,0:T(8,128)}) custom-call(bf16[1120,896]{1,0:T(8,128)(2,1)} %bitcast.32, bf16[1120,896]{1,0:T(8,128)(2,1)} %bitcast.33, f32[48,8,128]{2,1,0:T(8,128)} %bitcast.34), custom_call_target="tpu_custom_call" | custom-call | tf_op jit(solution)/shard_map/attend/pallas_call | solution.py:430
  88.2 14.4 %total3.1 = f32[16,3,8,128]{3,2,1,0:T(8,128)} custom-call(f32[16,3,8,128]{3,2,1,0:T(8,128)} %bitcast.36), custom_call_target="tpu_custom_call" | custom-call | tf_op jit(solution)/shard_map/total3/pallas_call | solution.py:370
  102.6 9.1 %features.1.r_0_ = bf16[2,896,1120]{2,1,0:T(8,128)(2,1)} custom-call(bf16[2,896,1120]{2,1,0:T(8,128)(2,1)} %get-tuple-element.20.r_0_, f32[48,8,128]{2,1,0:T(8,128)} %bitcast.35), custom_call_target="tpu_custom_call" | custom-call | tf_op jit(solution)/shard_map/features/pallas_call | solution.py:462
  111.8 64.9 %finish.1 = (f32[280,1120]{1,0:T(8,128)}, f32[280,1120]{1,0:T(8,128)}, bf16[2240,896]{1,0:T(8,128)(2,1)}) custom-call(bf16[2,896,1120]{2,1,0:T(8,128)(2,1)} %features.1.r_0_, bf16[8,280,896]{2,1,0:T(8,128)(2,1)} %bitcast.29, bf16[8,280,896]{2,1,0:T(8,128)(2,1)} %bitcast.30, bf16[2,2240,1120]{2,1,0:T(8,128)(2,1)} %bitcast.27), custom_call_target="tpu_custom_call" | custom-call | tf_op jit(solution)/shard_map/finish/pallas_call | solution.py:703
  176.7 0.0 copy-start.1
  176.7 0.0 copy-start
  176.7 4.6 %copy.13 = bf16[1,896,2240]{1,2,0:T(8,128)(2,1)} copy(bf16[1,896,2240]{1,2,0:T(8,128)(2,1)} %bitcast.31) | data formatting | bytes 8028160
  181.2 0.0 copy-done.1
  181.2 1.0 copy.14
  182.3 0.0 copy-done
  182.3 1.0 copy.15
Async XLA Ops:
  176.7 4.6 %copy-start.1 = (f32[280,1120]{1,0:T(8,128)S(1)}, f32[280,1120]{1,0:T(8,128)}, u32[]{:S(2)}) copy-start(f32[280,1120]{1,0:T(8,128)} %get-tuple-element.35) | copy-start | bytes 3763204
  176.7 5.6 %copy-start = (f32[280,1120]{1,0:T(8,128)S(1)}, f32[280,1120]{1,0:T(8,128)}, u32[]{:S(2)}) copy-start(f32[280,1120]{1,0:T(8,128)} %get-tuple-element.36) | copy-start | bytes 3763204

commit v3 on v2

--- a/solution.py
+++ b/solution.py
@@ -297,7 +297,54 @@
     return lane < width
 
 
-def project_kernel(width, tok_ref, w_ref, kv_ref, part_ref):
+SHARE = 3
+
+
+def peers_of(s):
+    places = [(s.sp + k) % 16 for k in range(16)]
+    return places, [{"img": s.img, "sp": p} for p in places]
+
+
+def share(ref, place):
+    return ref.at[pl.ds(place * SHARE, SHARE)]
+
+
+def total(s, part, sums, slots, sems):
+    places, devs = peers_of(s)
+    me = s.sp
+    out, back = [], []
+    for k in range(1, 16):
+        c = remote(share(part, places[k]), slots.at[k], sems.at[0, k], sems.at[1, k], devs[k])
+        c.start()
+        out.append(c)
+    acc = share(part, me)[...]
+    for k in range(1, 16):
+        out[k - 1].wait_recv()
+        acc = acc + slots[k]
+    mine = share(sums, me)
+    mine[...] = acc
+    for k in range(1, 16):
+        c = remote(mine, mine, sems.at[2, k], sems.at[3, k], devs[k])
+        c.start()
+        back.append(c)
+    for k in range(1, 16):
+        ref = share(sums, (me + 16 - k) % 16)
+        pltpu.make_async_copy(ref, ref, sems.at[3, k]).wait()
+    for c in out + back:
+        c.wait_send()
+
+
+def project_kernel(width, tok_ref, w_ref, kv_ref, out_ref, part, sums, slots, sems):
+    s = Seat()
+    g = pl.program_id(0)
+    bar = pltpu.get_barrier_semaphore()
+
+    @pl.when(g == 0)
+    def _():
+        for d in peers_of(s)[1][1:]:
+            pl.semaphore_signal(bar, inc=1, device_id=d, device_id_type=MESH)
+        part[45:48] = jnp.zeros((3, 8, LANE), F32)
+
     both = jnp.concatenate([w_ref[0], w_ref[1]], axis=1)
     acc = dot(tok_ref[...], both)
     ok = inside((acc.shape[0], LANE), width)
@@ -306,23 +353,30 @@
     kv_ref[0] = key
     kv_ref[1] = val
     put_state(
-        part_ref,
+        part.at[pl.ds(5 * g, 5)],
         fold(dot_t(key, val), same_head()),
         jnp.sum(key.astype(F32), axis=0, keepdims=True),
     )
+
+    @pl.when(g == pl.num_programs(0) - 1)
+    def _():
+        pl.semaphore_wait(bar, 15)
+        total(s, part, sums, slots, sems)
+        out_ref[...] = sums[...]
 
 
 def project(tok, w):
     count, depth = tok.shape
     width = w.shape[2]
     steps = pl.cdiv(width, LANE)
+    tiles = (48, 8, LANE)
     return pl.pallas_call(
         lambda *r: project_kernel(width, *r),
         name="project",
         grid=(steps,),
         out_shape=(
             jax.ShapeDtypeStruct((2, count, width), BF),
-            jax.ShapeDtypeStruct((48, 8, LANE), F32),
+            jax.ShapeDtypeStruct(tiles, F32),
         ),
         in_specs=[
             pl.BlockSpec((count, depth), lambda g: (0, 0)),
@@ -330,53 +384,16 @@
         ],
         out_specs=(
             pl.BlockSpec((2, count, LANE), lambda g: (0, 0, g)),
-            pl.BlockSpec((5, 8, LANE), lambda g: (g, 0, 0)),
+            pl.BlockSpec(tiles, lambda g: (0, 0, 0)),
         ),
-        compiler_params=params(),
+        scratch_shapes=[
+            pltpu.VMEM(tiles, F32),
+            pltpu.VMEM(tiles, F32),
+            pltpu.VMEM((16, SHARE, 8, LANE), F32),
+            DMA((4, 16)),
+        ],
+        compiler_params=params(2),
     )(tok, w)
-
-
-def total_kernel(part_ref, out_ref, slots, ssem, rsem, ssem2, rsem2):
-    s = Seat()
-    me = s.sp
-    peers = [(me + k) % 16 for k in range(16)]
-    devs = [{"img": s.img, "sp": p} for p in peers]
-    meet(devs[1:])
-    out = []
-    for k in range(1, 16):
-        c = remote(part_ref.at[peers[k]], slots.at[k], ssem.at[k], rsem.at[k], devs[k])
-        c.start()
-        out.append(c)
-    acc = part_ref[me]
-    for k in range(1, 16):
-        out[k - 1].wait_recv()
-        acc = acc + slots[k]
-    out_ref[me] = acc
-    back = []
-    for k in range(1, 16):
-        c = remote(out_ref.at[me], out_ref.at[me], ssem2.at[k], rsem2.at[k], devs[k])
-        c.start()
-        back.append(c)
-    for k in range(1, 16):
-        src = (me + 16 - k) % 16
-        pltpu.make_async_copy(out_ref.at[src], out_ref.at[src], rsem2.at[k]).wait()
-    for c in out + back:
-        c.wait_send()
-
-
-def total(part, cid):
-    four = part.reshape(16, 3, 8, LANE)
-    vm = pl.BlockSpec(memory_space=pltpu.VMEM)
-    got = pl.pallas_call(
-        total_kernel,
-        name=f"total{cid}",
-        out_shape=jax.ShapeDtypeStruct(four.shape, F32),
-        in_specs=[vm],
-        out_specs=vm,
-        scratch_shapes=[pltpu.VMEM(four.shape, F32)] + [DMA((16,))] * 4,
-        compiler_params=params(cid),
-    )(four)
-    return got.reshape(48, 8, LANE)
 
 
 def dot_r(a, b):
@@ -442,43 +459,16 @@
     )(q, g, state)
 
 
-def features_kernel(tok_img, kv_ref, st_ref, d_ref):
-    mask = same_head()
-    state = st_ref[0:4].reshape(32, LANE) * tok_img
-    row = st_ref[4][0:1] * tok_img
-    gs = unfold(state, mask)
-    gh, gl = split(gs)
-    th, tl = split(jnp.transpose(gs))
-    key, val = kv_ref[0], kv_ref[1]
-    dk = dot(jnp.concatenate([val, val], axis=1), jnp.concatenate([th, tl], axis=0)) + row
-    d_ref[0] = jnp.where(key > 0, dk, 0.0).astype(BF)
-    dv = dot(jnp.concatenate([key, key], axis=1), jnp.concatenate([gh, gl], axis=0))
-    d_ref[1] = dv.astype(BF)
-
-
-def features(kv, state, tok_img):
-    _, count, width = kv.shape
-    cols = pl.BlockSpec((2, count, LANE), lambda i: (0, 0, i))
-    return pl.pallas_call(
-        lambda *r: features_kernel(float(tok_img), *r),
-        name="features",
-        grid=(pl.cdiv(width, LANE),),
-        out_shape=jax.ShapeDtypeStruct(kv.shape, BF),
-        in_specs=[cols, pl.BlockSpec((5, 8, LANE), lambda i: (i, 0, 0))],
-        out_specs=cols,
-        compiler_params=params(),
-    )(kv, state)
-
-
 PIECE = 72
 OFFS = (0, 72, 144, 208)
 CUT = 640
+SPLIT = 512
 BAND = 448
 
 
-def finish_kernel(scale, d_ref, tok_ref, tok2_ref, w_ref, ok_ref, ov_ref, dt_ref, cat, dcat, dboth,
-                  gp, relay, final, comb, res1, relay2, final2, res2, zbuf, fin, wbuf, tbuf,
-                  ssem, rsem, lsem, csem, wsem, osem):
+def finish_kernel(scale, tok_img, part_ref, kv_ref, tok_ref, tok2_ref, w_ref, ok_ref, ov_ref, dt_ref,
+                  cat, dcat, dboth, kvb, sums, slots, gp, relay, final, comb, res1, relay2, final2,
+                  res2, zbuf, fin, wbuf, tbuf, ssem, rsem, lsem, csem, wsem, osem, tsem):
     s = Seat()
     core = s.core
     x_r, x_l, y_r, y_l = s.at(dx=1), s.at(dx=-1), s.at(dy=1), s.at(dy=-1)
@@ -487,17 +477,16 @@
     me1 = s.x * (1 - core) + s.y * core
     me2 = s.y * (1 - core) + s.x * core
     across, beside, partner = s.across(), s.beside(), s.partner()
-    count = d_ref.shape[1]
+    count, width = kv_ref.shape[1:]
 
     def loader(src, dst, i):
         return pltpu.make_async_copy(src, dst, lsem.at[i])
 
     lo, up = pl.ds(0, count), pl.ds(count, count)
     ld = [
-        loader(d_ref.at[core], dcat.at[lo], 0),
+        loader(kv_ref, kvb, 0),
         loader(tok_ref, cat.at[:, :, lo], 1),
         loader(tok2_ref, cat.at[:, :, up], 2),
-        loader(d_ref, dboth, 3),
     ]
     for c in ld:
         c.start()
@@ -509,9 +498,45 @@
 
     band_load(0).start()
     band_load(1).start()
-    meet((x_r, x_l, y_r, y_l, across, beside, partner))
-    swap = remote(d_ref.at[1 - core], dcat.at[up], ssem.at[22], rsem.at[18], partner)
-    swap.start()
+    meet([x_r, x_l, across] + peers_of(s)[1][1:])
+    total(s, part_ref, sums, slots, tsem)
+    ld[0].wait()
+    mask = same_head()
+
+    def swap(i):
+        at = pl.ds((0, SPLIT)[i], (SPLIT, width - SPLIT)[i])
+        return remote(
+            dboth.at[1 - core, :, at], dcat.at[up, at], ssem.at[22 + i], rsem.at[18 + i], partner
+        )
+
+    def features(g, at, n):
+        gs = unfold(sums[pl.ds(5 * g, 4)].reshape(32, LANE) * tok_img, mask)[:n, :n]
+        row = sums[5 * g + 4][0:1, :n] * tok_img
+        gh, gl = split(gs)
+        th, tl = split(jnp.transpose(gs))
+        key, val = kvb[0, :, at], kvb[1, :, at]
+
+        def twice(a, h, l):
+            if n < LANE:
+                return dot(a, h) + dot(a, l)
+            return dot(jnp.concatenate([a, a], axis=1), jnp.concatenate([h, l], axis=0))
+
+        dk = jnp.where(key > 0, twice(val, th, tl) + row, 0.0).astype(BF)
+        dv = twice(key, gh, gl).astype(BF)
+        dboth[0, :, at] = dk
+        dboth[1, :, at] = dv
+        dcat[lo, at] = jnp.where(core == 0, dk.astype(F32), dv.astype(F32)).astype(BF)
+
+    def tile(g, _):
+        features(g, pl.ds(pl.multiple_of(g * LANE, LANE), LANE), LANE)
+        return 0
+
+    lax.fori_loop(0, SPLIT // LANE, tile, 0)
+    swap(0).start()
+    lax.fori_loop(SPLIT // LANE, width // LANE, tile, 0)
+    tail = width - width // LANE * LANE
+    features(width // LANE, pl.ds(width - tail, tail), tail)
+    swap(1).start()
 
     pending = []
 
@@ -534,8 +559,6 @@
         return pltpu.make_async_copy(tbuf.at[i % 2], dt_ref.at[at], osem.at[i])
 
     def band(i):
-        if i == 0:
-            ld[3].wait()
         band_load(i).wait()
         if i >= 2:
             bands_out(i - 2).wait()
@@ -595,9 +618,10 @@
         add(comb.at[1], gp.at[1, nxt(me1, 3)], relay.at[1])
         copy(comb.at[1], final.at[1, 1], 5, left1).start()
 
-    for c in ld[:3]:
+    for c in ld[1:]:
         c.wait()
-    swap.wait()
+    swap(0).wait()
+    swap(1).wait()
     for h, dx in ((0, 2), (1, 2), (1, 1), (0, 3), (0, 1), (1, 3)):
         shard(h, dx)
 
@@ -693,24 +717,27 @@
         ref[pl.ds(216, 64)] = fin[i, 3].astype(F32)[8:] * scale
 
 
-def finish(d, tok, tok2, w, scale):
-    _, count, width = d.shape
+def finish(part, kv, tok, tok2, w, scale, tok_img):
+    _, count, width = kv.shape
     depth = tok.shape[0]
     rows = depth // 8
     vm = pl.BlockSpec(memory_space=pltpu.VMEM)
     hbm = pl.BlockSpec(memory_space=pl.ANY)
     p = (PIECE, width)
     return pl.pallas_call(
-        lambda *r: finish_kernel(scale, *r),
+        lambda *r: finish_kernel(scale, tok_img, *r),
         name="finish",
         out_shape=(jax.ShapeDtypeStruct((rows, width), F32),) * 2
         + (jax.ShapeDtypeStruct((depth, count), BF),),
-        in_specs=[hbm] * 4,
+        in_specs=[vm] + [hbm] * 4,
         out_specs=(vm, vm, hbm),
         scratch_shapes=[
             pltpu.VMEM((8, rows, 2 * count), BF),
             pltpu.VMEM((2 * count, width), BF),
             pltpu.VMEM((2, count, width), BF),
+            pltpu.VMEM((2, count, width), BF),
+            pltpu.VMEM(part.shape, F32),
+            pltpu.VMEM((16, SHARE, 8, LANE), F32),
             pltpu.VMEM((2, 4, 4) + p, BF),
             pltpu.VMEM((2, 4) + p, BF),
             pltpu.VMEM((2, 2, 4) + p, BF),
@@ -723,10 +750,10 @@
             pltpu.VMEM((2, 4) + p, BF),
             pltpu.VMEM((2, 2, BAND, width), BF),
             pltpu.VMEM((2, BAND, count), BF),
-            DMA((23,)), DMA((19,)), DMA((4,)), DMA((4,)), DMA((5,)), DMA((5,)),
+            DMA((24,)), DMA((20,)), DMA((3,)), DMA((4,)), DMA((5,)), DMA((5,)), DMA((4, 16)),
         ],
         compiler_params=params(5),
-    )(d, tok.reshape(8, rows, count), tok2.reshape(8, rows, count), w)
+    )(part, kv, tok.reshape(8, rows, count), tok2.reshape(8, rows, count), w)
 
 
 def body(tokens, queries, w_key, w_value, cotangent):
@@ -737,12 +764,10 @@
     images = lax.axis_size("img")
     w4, tok2, tok_t = gather(w_key, w_value, tok)
     w = w4.reshape(2, depth, width)
-    kv, part = project(tok_t, w)
-    state = total(part, 2)
-    att, dq, gpart = attend(jnp.transpose(queries[0]), jnp.transpose(cotangent[0]), state)
-    gstate = total(gpart, 3)
-    d = features(kv, gstate, tok_img)
-    dwk, dwv, dt = finish(d, tok, tok2, w, float((images * tok_img) ** -0.5))
+    kv, state = project(tok_t, w)
+    att, dq, part = attend(jnp.transpose(queries[0]), jnp.transpose(cotangent[0]), state)
+    scale = float((images * tok_img) ** -0.5)
+    dwk, dwv, dt = finish(part, kv, tok, tok2, w, scale, float(tok_img))
     return jnp.transpose(att)[None], jnp.transpose(dt)[None], jnp.transpose(dq)[None], dwk, dwv
 
 

time: 184 us -> 173 us (0.940)
  Pallas kernels: 176 us -> 164 us
    pallas_call x4 -> x1, Pallas kernels: 104 us -> 80 us  [finish(): pl.pallas_call(lambda *r: finish_kernel(scale, tok_img, *r), name='finish...]
    pallas_call x1, Pallas kernels: 16.7 us -> 28.1 us  [project(): pl.pallas_call(lambda *r: project_kernel(width, *r), name='project', grid...]
where the time goes in v3:
time: 173 us; the launch traced here: 172 us
  Pallas kernels  164 us (95%)
  local copies, waits for them, and re-layouts  7.33 us (4%)
    pallas_call x1, Pallas kernels, finish(): pl.pallas_call(lambda *r: finish_kernel(scale, tok_img, *r), name='finish...  80 us
    pallas_call x1, Pallas kernels, gather(): pl.pallas_call(gather_kernel, name='gather', out_shape=(jax.ShapeDtypeStr...  43.7 us
    pallas_call x1, Pallas kernels, project(): pl.pallas_call(lambda *r: project_kernel(width, *r), name='project', grid...  28.1 us
    pallas_call x1, Pallas kernels, attend(): pl.pallas_call(lambda *r: attend_kernel(width, *r), name='attend', grid=(...  11.9 us
    unnamed x7, local copies, waits for them, and re-layouts  7.33 us

profile of v3, /device:TPU:1, one launch (start us, length us, event | category | flops | bytes accessed | tf_op | source)
XLA Modules:
  0.0 171.7 jit_solution(5344148854612321780)
XLA Ops:
  0.6 43.7 %gather.1 = (bf16[2,8,280,1120]{3,2,1,0:T(8,128)(2,1)}, bf16[2240,896]{1,0:T(8,128)(2,1)}, bf16[896,2240]{1,0:T(8,128)(2,1)}) custom-call(bf16[280,1120]{1,0:T(8,128)(2,1)} %wk_ref.1, bf16[280,1120]{1,0:T(8,128)(2,1)} %wv_ref.1, bf16[2240,896]{1,0:T(8,128)(2,1)} %bitcast.24), custom_call_target="tpu_custom_call" | custom-call | tf_op jit(solution)/shard_map/gather/pallas_call | solution.py:242
  44.4 28.1 %project.1 = (bf16[2,896,1120]{2,1,0:T(8,128)(2,1)}, f32[48,8,128]{2,1,0:T(8,128)}) custom-call(bf16[896,2240]{1,0:T(8,128)(2,1)} %get-tuple-element.16.r_0_, bf16[2,2240,1120]{2,1,0:T(8,128)(2,1)} %bitcast.22), custom_call_target="tpu_custom_call" | custom-call | tf_op jit(solution)/shard_map/project/pallas_call | solution.py:373
  72.5 11.9 %attend.1 = (bf16[1120,896]{1,0:T(8,128)(2,1)}, bf16[1120,896]{1,0:T(8,128)(2,1)}, f32[48,8,128]{2,1,0:T(8,128)}) custom-call(bf16[1120,896]{1,0:T(8,128)(2,1)} %bitcast.28, bf16[1120,896]{1,0:T(8,128)(2,1)} %bitcast.29, f32[48,8,128]{2,1,0:T(8,128)} %get-tuple-element.18.r_2_), custom_call_target="tpu_custom_call" | custom-call | tf_op jit(solution)/shard_map/attend/pallas_call | solution.py:447
  84.3 80.0 %finish.1 = (f32[280,1120]{1,0:T(8,128)}, f32[280,1120]{1,0:T(8,128)}, bf16[2240,896]{1,0:T(8,128)(2,1)}) custom-call(f32[48,8,128]{2,1,0:T(8,128)} %get-tuple-element.20.r_0_, bf16[2,896,1120]{2,1,0:T(8,128)(2,1)} %get-tuple-element.21.r_1_, bf16[8,280,896]{2,1,0:T(8,128)(2,1)} %bitcast.25, bf16[8,280,896]{2,1,0:T(8,128)(2,1)} %bitcast.26, ...), custom_call_target="tpu_custom_call" | custom-call | tf_op jit(solution)/shard_map/finish/pallas_call | solution.py:727
  164.4 0.0 copy-start.1
  164.4 4.5 %copy.13 = bf16[1,896,2240]{1,2,0:T(8,128)(2,1)} copy(bf16[1,896,2240]{1,2,0:T(8,128)(2,1)} %bitcast.27) | data formatting | bytes 8028160
  168.9 0.0 copy-done.1
  168.9 0.0 copy-start
  168.9 1.0 copy.14
  169.9 0.7 copy-done
  170.7 1.0 copy.15
Async XLA Ops:
  164.4 4.5 %copy-start.1 = (f32[280,1120]{1,0:T(8,128)S(1)}, f32[280,1120]{1,0:T(8,128)}, u32[]{:S(2)}) copy-start(f32[280,1120]{1,0:T(8,128)} %get-tuple-element.35) | copy-start | bytes 3763204
  168.9 1.8 %copy-start = (f32[280,1120]{1,0:T(8,128)S(1)}, f32[280,1120]{1,0:T(8,128)}, u32[]{:S(2)}) copy-start(f32[280,1120]{1,0:T(8,128)} %get-tuple-element.36) | copy-start | bytes 3763204

commit v4 on v3

--- a/solution.py
+++ b/solution.py
@@ -67,10 +67,16 @@
 L0, L1, R0, R1, O0, O1, YL0, YR0, YO0, YL1, YR1, YO1, ZM0, ZM1, ZN0, ZN1 = range(16)
 
 
-def gather_kernel(wk_ref, wv_ref, tok_ref, out, tok_out, tok_t, w_ref, tin, tup, ssem, rsem, csem,
-                  lsem, tsem, usem):
+PHASES = ((0, 640), (640, 480))
+READY = 5
+
+
+def gather_kernel(wk_ref, wv_ref, tok_ref, out, tok_out, kv_out, state_out, w_ref, tin, tup, wt, wlast,
+                  kvb, part, sums, slots, ssem, rsem, csem, lsem, tsem, usem, wsem, sems):
     s = Seat()
     m = s.y % 2
+    width = wk_ref.shape[1]
+    rows = wk_ref.shape[0]
     right, left = s.at(dx=1), s.at(dx=-1)
     up, down = s.at(dy=1), s.at(dy=-1)
     partner, across = s.partner(), s.across()
@@ -81,70 +87,114 @@
     for c in loads:
         c.start()
     read.start()
-    meet((right, left, up, down, partner, across))
+    meet([right, left, across] + peers_of(s)[1][1:])
     for c in loads:
         c.wait()
 
-    def part(mat, shard, h):
-        return out.at[mat, shard, pl.ds(HALVES[h][0], HALVES[h][1])]
-
-    def mine(mat, h):
-        return w_ref.at[mat, pl.ds(HALVES[h][0], HALVES[h][1])]
-
-    def place(k, core):
+    def spot(mat, shard, h, p):
+        row = pl.multiple_of(shard * rows + HALVES[h][0], 8)
+        return out.at[mat, pl.ds(row, HALVES[h][1]), pl.ds(*PHASES[p])]
+
+    def mine(mat, h, p):
+        return w_ref.at[mat, pl.ds(*HALVES[h]), pl.ds(*PHASES[p])]
+
+    def place(k, core, p):
         hi = (s.zhi + core) % 2
         if k >= ZM0:
-            return part(m if k < ZN0 else 1 - m, (1 - s.zhi) * 4 + s.x, (k - ZM0) % 2)
+            return spot(m if k < ZN0 else 1 - m, (1 - s.zhi) * 4 + s.x, (k - ZM0) % 2, p)
         dx, h = {
             L0: (3, 0), L1: (3, 1), R0: (1, 0), R1: (1, 1), O0: (2, 0), O1: (2, 1),
             YL0: (3, 0), YR0: (1, 0), YO0: (2, 0), YL1: (3, 1), YR1: (1, 1), YO1: (2, 1),
         }[k]
-        return part(m if k < YL0 else 1 - m, hi * 4 + (s.x + dx) % 4, h)
-
-    swap = remote(tok_ref, tok_out, tsem.at[0], tsem.at[1], partner)
-    owns = [
-        pltpu.make_async_copy(w_ref.at[i], out.at[i, s.img], lsem.at[i]) for i in range(2)
-    ]
-    sent = []
-
-    def send(src, dst, k, device, sems, start=True):
-        slot = len(sent)
-        c = remote(src, dst, ssem.at[slot], sems.at[k], device)
-        sent.append(c)
-        if start:
-            c.start()
-        return c
+        return spot(m if k < YL0 else 1 - m, hi * 4 + (s.x + dx) % 4, h, p)
 
     is0, is1 = s.core == 0, s.core == 1
     hi = (s.zhi + s.core) % 2
     seed = hi * 4 + s.x
-
-    zs = [
-        send(mine(mat, h), part(mat, s.img, h), k, across, rsem, False)
-        for k, mat, h in ((ZM0, m, 0), (ZM1, m, 1), (ZN0, 1 - m, 0), (ZN1, 1 - m, 1))
-    ]
-    first = [
-        (send(mine(m, h), part(m, s.img, h), k, d, rsem, False), h)
-        for h, k, d in ((0, L0, right), (1, R1, left), (1, L1, right), (0, R0, left))
-    ]
-    second = [
-        (remote(part(m, seed, h), part(m, seed, h), ssem.at[4 + i], rsem.at[k], d), h)
-        for i, (h, k, d) in enumerate(((0, L0, right), (1, R1, left), (1, L1, right), (0, R0, left)))
-    ]
+    always, second = [], []
+
+    def new(src, dst, k, p, device, sem, only1=False):
+        slot = len(always) + len(second)
+        c = remote(src, dst, ssem.at[slot], sem.at[p, k], device)
+        (second if only1 else always).append(c)
+        return c
+
+    zs, seeds0, seeds1, onward, chips = {}, {}, {}, {}, {}
+    for p in range(2):
+        for k, mat, h in ((ZM0, m, 0), (ZM1, m, 1), (ZN0, 1 - m, 0), (ZN1, 1 - m, 1)):
+            zs[k, p] = new(mine(mat, h, p), spot(mat, s.img, h, p), k, p, across, rsem, True)
+        for i, (h, k, d) in enumerate(((0, L0, right), (1, R1, left), (1, L1, right), (0, R0, left))):
+            slot = ssem.at[len(always) + len(second)]
+            there = spot(m, seed, h, p)
+            seeds1[i, p] = remote(there, there, slot, rsem.at[p, k], d)
+            seeds0[i, p] = new(mine(m, h, p), spot(m, s.img, h, p), k, p, d, rsem)
+        for k, to, d in (
+            (L0, O0, right), (R1, O1, left),
+            (L0, YL0, up), (R0, YR0, up), (O0, YO0, up),
+            (L1, YL1, down), (R1, YR1, down), (O1, YO1, down),
+        ):
+            ref = place(k, s.core, p)
+            onward.setdefault((k, p), []).append(new(ref, ref, to, p, d, rsem))
+        for k in range(16):
+            ref = place(k, s.core, p)
+            chips[k, p] = new(ref, ref, k, p, partner, csem, k >= ZM0)
+
+    def got(k, p, sem, core):
+        ref = place(k, core, p)
+        pltpu.make_async_copy(ref, ref, sem.at[p, k]).wait()
+
+    def arrive(p, *ks):
+        for k in ks:
+            got(k, p, rsem, s.core)
+            for c in onward.get((k, p), ()):
+                c.start()
+            chips[k, p].start()
+
+    def across_in(p, *ks):
+        @pl.when(is1)
+        def _():
+            for k in ks:
+                arrive(p, k)
+                if k in (ZM0, ZM1):
+                    h = k - ZM0
+                    for i in ((0, 3), (1, 2))[h]:
+                        seeds1[i, p].start()
+
+    def seed0(p, *which):
+        @pl.when(is0)
+        def _():
+            for i in which:
+                seeds0[i, p].start()
+
+    def settled(p):
+        for k in range(ZM0):
+            got(k, p, csem, 1 - s.core)
+
+        @pl.when(is0)
+        def _():
+            for k in range(ZM0, 16):
+                got(k, p, csem, 1)
 
     @pl.when(is1)
     def _():
-        for c in zs:
-            c.start()
-
-    @pl.when(is0)
-    def _():
-        for c, _h in first:
-            c.start()
-
+        for k, p in (
+            (ZM0, 0), (ZM1, 0), (ZM0, 1), (ZM1, 1), (ZN0, 0), (ZN1, 0), (ZN0, 1), (ZN1, 1)
+        ):
+            zs[k, p].start()
+
+    seed0(0, 0, 1, 2, 3)
+    seed0(1, 0, 1)
+    swap = remote(tok_ref, tok_out, tsem.at[0], tsem.at[1], partner)
+    owns = [
+        pltpu.make_async_copy(
+            w_ref.at[i],
+            out.at[i, pl.ds(pl.multiple_of(s.img * rows, 8), rows)],
+            lsem.at[i],
+        )
+        for i in range(2)
+    ]
     for c in owns:
         c.start()
-    swap.start()
     read.wait()
     depth = tok_ref.shape[0]
     whole = depth // ROWS
@@ -158,102 +208,139 @@
     lax.fori_loop(0, whole, flip, 0)
     at = pl.ds(whole * ROWS, rest)
     tup[:, at] = jnp.transpose(tin[at])
-    write = pltpu.make_async_copy(tup, tok_t, usem.at[1])
-    write.start()
-
-    def got(k, sems, core):
-        ref = place(k, core)
-        pltpu.make_async_copy(ref, ref, sems.at[k]).wait()
-
-    chips = {}
-
-    def onchip(k, start=True):
-        ref = place(k, s.core)
-        chips[k] = send(ref, ref, k, partner, csem, start)
-
-    for k in (ZM0, ZM1, ZN0, ZN1):
-        onchip(k, False)
+    across_in(0, ZM0, ZM1)
+    across_in(1, ZM0, ZM1)
+    arrive(0, L0, R1)
+    seed0(1, 2, 3)
+    arrive(0, L1, R0, YL0, YR1)
+    swap.start()
+    arrive(1, L0, R1)
+    across_in(0, ZN0, ZN1)
+    arrive(0, O0, O1, YR0, YL1)
+    arrive(1, L1, R0)
+    arrive(0, YO0, YO1)
+    settled(0)
+    for c in owns:
+        c.wait()
+
+    def tile_load(i):
+        at = pl.ds(pl.multiple_of(i * LANE, LANE), LANE)
+        slot = i % 2
+        return [
+            pltpu.make_async_copy(
+                out.at[j, :, at], wt.at[slot, :, pl.ds(j * LANE, LANE)], wsem.at[slot]
+            )
+            for j in range(2)
+        ]
+
+    full = width // LANE
+    tail = width - full * LANE
+    last = pltpu.make_async_copy(out.at[:, :, pl.ds(full * LANE, tail)], wlast, usem.at[1])
+    mask = same_head()
+    part[45:48] = jnp.zeros((3, 8, LANE), F32)
+    for c in tile_load(0):
+        c.start()
+
+    def keep(i, key, val, at):
+        kvb[0, :, at] = key
+        kvb[1, :, at] = val
+        n = key.shape[1]
+        state = dot_t(key, val)
+        row = jnp.sum(key.astype(F32), axis=0, keepdims=True)
+        if n < LANE:
+            state = jnp.where(mask[:n, :n], state, 0.0)
+            state = state[0:32] + state[32:64] + state[64:96]
+            state = jnp.concatenate([state, jnp.zeros((32, LANE - n), F32)], axis=1)
+            row = jnp.concatenate([row, jnp.zeros((1, LANE - n), F32)], axis=1)
+        else:
+            state = fold(state, mask)
+        put_state(part.at[pl.ds(5 * i, 5)], state, row)
+
+    def tile(i, _):
+        @pl.when(i == 0)
+        def _():
+            arrive(1, O0, O1, YL0, YR1)
+
+        @pl.when(i == 1)
+        def _():
+            across_in(1, ZN0, ZN1)
+            arrive(1, YR0, YL1)
+
+        @pl.when(i == 2)
+        def _():
+            arrive(1, YO0, YO1)
+
+        @pl.when(i == READY)
+        def _():
+            settled(1)
+            for c in tile_load(READY):
+                c.start()
+            last.start()
+
+        slot = i % 2
+        pltpu.make_async_copy(wt.at[slot], wt.at[slot], wsem.at[slot]).wait()
+
+        @pl.when(jnp.logical_and(i + 1 < full, i + 1 != READY))
+        def _():
+            for c in tile_load(i + 1):
+                c.start()
+
+        acc = dot(tup[...], wt[slot])
+        key = jnp.maximum(acc[:, :LANE], 0.0).astype(BF)
+        keep(i, key, acc[:, LANE:].astype(BF), pl.ds(pl.multiple_of(i * LANE, LANE), LANE))
+        return 0
+
+    lax.fori_loop(0, full, tile, 0)
+    last.wait()
+    pad = jnp.zeros((depth, LANE - tail), BF)
+    acc = dot(tup[...], jnp.concatenate([wlast[0], pad, wlast[1]], axis=1))
+    key = jnp.maximum(acc[:, :tail], 0.0).astype(BF)
+    keep(full, key, acc[:, LANE : LANE + tail].astype(BF), pl.ds(full * LANE, tail))
+    kv_write = pltpu.make_async_copy(kvb, kv_out, usem.at[2])
+    kv_write.start()
+    total(s, part, sums, slots, sems)
+    state_out[...] = sums[...]
+    for c in always:
+        c.wait_send()
 
     @pl.when(is1)
     def _():
-        for h, k in ((0, ZM0), (1, ZM1)):
-            got(k, rsem, s.core)
-            for c, ch in second:
-                if ch == h:
-                    c.start()
-            chips[k].start()
-
-    def arrive(k):
-        got(k, rsem, s.core)
-        ref = place(k, s.core)
-        if k == L0:
-            send(ref, ref, O0, right, rsem)
-        if k == R1:
-            send(ref, ref, O1, left, rsem)
-        for a, b, d in (
-            (L0, YL0, up), (R0, YR0, up), (O0, YO0, up),
-            (L1, YL1, down), (R1, YR1, down), (O1, YO1, down),
-        ):
-            if k == a:
-                send(ref, ref, b, d, rsem)
-        onchip(k)
-
-    for k in (L0, R1, L1, R0, YL0, YR1):
-        arrive(k)
-
-    @pl.when(is1)
-    def _():
-        for k in (ZN0, ZN1):
-            got(k, rsem, s.core)
-            chips[k].start()
-
-    for k in (O0, O1, YR0, YL1, YO0, YO1):
-        arrive(k)
-
-    for k in range(ZM0):
-        got(k, csem, 1 - s.core)
-
-    @pl.when(is0)
-    def _():
-        for k in (ZM0, ZM1, ZN0, ZN1):
-            got(k, csem, 1 - s.core)
-
-    conditional = {id(c) for c in zs} | {id(chips[k]) for k in (ZM0, ZM1, ZN0, ZN1)}
-    for c in sent:
-        if id(c) not in conditional:
+        for c in second:
             c.wait_send()
 
-    @pl.when(is1)
-    def _():
-        for c in zs:
-            c.wait_send()
-        for k in (ZM0, ZM1, ZN0, ZN1):
-            chips[k].wait_send()
-
-    for c in owns:
-        c.wait()
     swap.wait()
-    write.wait()
+    kv_write.wait()
 
 
 def gather(wk, wv, tok):
     rows, cols = wk.shape
+    depth, count = tok.shape
     hbm = pl.BlockSpec(memory_space=pl.ANY)
+    vm = pl.BlockSpec(memory_space=pltpu.VMEM)
+    tiles = (48, 8, LANE)
     return pl.pallas_call(
         gather_kernel,
         name="gather",
         out_shape=(
-            jax.ShapeDtypeStruct((2, 8, rows, cols), BF),
+            jax.ShapeDtypeStruct((2, depth, cols), BF),
             jax.ShapeDtypeStruct(tok.shape, BF),
-            jax.ShapeDtypeStruct(tok.shape[::-1], BF),
+            jax.ShapeDtypeStruct((2, count, cols), BF),
+            jax.ShapeDtypeStruct(tiles, F32),
         ),
         in_specs=[hbm] * 3,
-        out_specs=(hbm,) * 3,
+        out_specs=(hbm, hbm, hbm, vm),
         scratch_shapes=[
             pltpu.VMEM((2, rows, cols), BF),
             pltpu.VMEM(tok.shape, BF),
             pltpu.VMEM(tok.shape[::-1], BF),
-            DMA((40,)), DMA((16,)), DMA((16,)), DMA((4,)), DMA((2,)), DMA((2,)),
+            pltpu.VMEM((2, depth, 2 * LANE), BF),
+            pltpu.VMEM((2, depth, cols % LANE), BF),
+            pltpu.VMEM((2, count, cols), BF),
+            pltpu.VMEM(tiles, F32),
+            pltpu.VMEM(tiles, F32),
+            pltpu.VMEM((16, SHARE, 8, LANE), F32),
+            DMA((64,)), DMA((2, 16)), DMA((2, 16)), DMA((4,)), DMA((2,)), DMA((3,)), DMA((2,)),
+            DMA((4, 16)),
         ],
         compiler_params=params(1),
     )(wk, wv, tok)
@@ -290,11 +377,6 @@
 
 def dot_t(a, b):
     return lax.dot_general(a, b, (((0,), (0,)), ((), ())), preferred_element_type=F32)
-
-
-def inside(shape, width):
-    lane = lax.broadcasted_iota(jnp.int32, shape, 1) + pl.program_id(0) * LANE
-    return lane < width
 
 
 SHARE = 3
@@ -332,68 +414,6 @@
         pltpu.make_async_copy(ref, ref, sems.at[3, k]).wait()
     for c in out + back:
         c.wait_send()
-
-
-def project_kernel(width, tok_ref, w_ref, kv_ref, out_ref, part, sums, slots, sems):
-    s = Seat()
-    g = pl.program_id(0)
-    bar = pltpu.get_barrier_semaphore()
-
-    @pl.when(g == 0)
-    def _():
-        for d in peers_of(s)[1][1:]:
-            pl.semaphore_signal(bar, inc=1, device_id=d, device_id_type=MESH)
-        part[45:48] = jnp.zeros((3, 8, LANE), F32)
-
-    both = jnp.concatenate([w_ref[0], w_ref[1]], axis=1)
-    acc = dot(tok_ref[...], both)
-    ok = inside((acc.shape[0], LANE), width)
-    key = jnp.where(ok, jnp.maximum(acc[:, :LANE], 0.0), 0.0).astype(BF)
-    val = jnp.where(ok, acc[:, LANE:], 0.0).astype(BF)
-    kv_ref[0] = key
-    kv_ref[1] = val
-    put_state(
-        part.at[pl.ds(5 * g, 5)],
-        fold(dot_t(key, val), same_head()),
-        jnp.sum(key.astype(F32), axis=0, keepdims=True),
-    )
-
-    @pl.when(g == pl.num_programs(0) - 1)
-    def _():
-        pl.semaphore_wait(bar, 15)
-        total(s, part, sums, slots, sems)
-        out_ref[...] = sums[...]
-
-
-def project(tok, w):
-    count, depth = tok.shape
-    width = w.shape[2]
-    steps = pl.cdiv(width, LANE)
-    tiles = (48, 8, LANE)
-    return pl.pallas_call(
-        lambda *r: project_kernel(width, *r),
-        name="project",
-        grid=(steps,),
-        out_shape=(
-            jax.ShapeDtypeStruct((2, count, width), BF),
-            jax.ShapeDtypeStruct(tiles, F32),
-        ),
-        in_specs=[
-            pl.BlockSpec((count, depth), lambda g: (0, 0)),
-            pl.BlockSpec((2, depth, LANE), lambda g: (0, 0, g)),
-        ],
-        out_specs=(
-            pl.BlockSpec((2, count, LANE), lambda g: (0, 0, g)),
-            pl.BlockSpec(tiles, lambda g: (0, 0, 0)),
-        ),
-        scratch_shapes=[
-            pltpu.VMEM(tiles, F32),
-            pltpu.VMEM(tiles, F32),
-            pltpu.VMEM((16, SHARE, 8, LANE), F32),
-            DMA((4, 16)),
-        ],
-        compiler_params=params(2),
-    )(tok, w)
 
 
 def dot_r(a, b):
@@ -762,9 +782,7 @@
     width = w_key.shape[1]
     tok_img = count * lax.axis_size("sp")
     images = lax.axis_size("img")
-    w4, tok2, tok_t = gather(w_key, w_value, tok)
-    w = w4.reshape(2, depth, width)
-    kv, state = project(tok_t, w)
+    w, tok2, kv, state = gather(w_key, w_value, tok)
     att, dq, part = attend(jnp.transpose(queries[0]), jnp.transpose(cotangent[0]), state)
     scale = float((images * tok_img) ** -0.5)
     dwk, dwv, dt = finish(part, kv, tok, tok2, w, scale, float(tok_img))

time: 173 us -> 166 us (0.960)
  Pallas kernels: 164 us -> 158 us
    pallas_call x1 -> x0, Pallas kernels: 28.1 us -> none  [project(): pl.pallas_call(lambda *r: project_kernel(width, *r), name='project', grid...]
    pallas_call x1, Pallas kernels: 43.7 us -> 67.7 us  [gather(): pl.pallas_call(gather_kernel, name='gather', out_shape=(jax.ShapeDtypeStr...]
where the time goes in v4:
time: 166 us
  Pallas kernels  158 us (95%)
  local copies, waits for them, and re-layouts  7.33 us (4%)
    pallas_call x1, Pallas kernels, finish(): pl.pallas_call(lambda *r: finish_kernel(scale, tok_img, *r), name='finish...  78.3 us
    pallas_call x1, Pallas kernels, gather(): pl.pallas_call(gather_kernel, name='gather', out_shape=(jax.ShapeDtypeStr...  67.7 us
    pallas_call x1, Pallas kernels, attend(): pl.pallas_call(lambda *r: attend_kernel(width, *r), name='attend', grid=(...  11.8 us
    unnamed x7, local copies, waits for them, and re-layouts  7.33 us

profile of v4, /device:TPU:1, one launch (start us, length us, event | category | flops | bytes accessed | tf_op | source)
XLA Modules:
  0.0 165.9 jit_solution(12263969484996074590)
XLA Ops:
  0.6 67.7 %gather.1 = (bf16[2,2240,1120]{2,1,0:T(8,128)(2,1)}, bf16[2240,896]{1,0:T(8,128)(2,1)}, bf16[2,896,1120]{2,1,0:T(8,128)(2,1)}, f32[48,8,128]{2,1,0:T(8,128)}) custom-call(bf16[280,1120]{1,0:T(8,128)(2,1)} %wk_ref.1, bf16[280,1120]{1,0:T(8,128)(2,1)} %wv_ref.1, bf16[2240,896]{1,0:T(8,128)(2,1)} %bitcast.21), custom_call_target="tpu_custom_call" | custom-call | tf_op jit(solution)/shard_map/gather/pallas_call | solution.py:321
  68.4 11.8 %attend.1 = (bf16[1120,896]{1,0:T(8,128)(2,1)}, bf16[1120,896]{1,0:T(8,128)(2,1)}, f32[48,8,128]{2,1,0:T(8,128)}) custom-call(bf16[1120,896]{1,0:T(8,128)(2,1)} %bitcast.25, bf16[1120,896]{1,0:T(8,128)(2,1)} %bitcast.26, f32[48,8,128]{2,1,0:T(8,128)} %get-tuple-element.15.r_2_), custom_call_target="tpu_custom_call" | custom-call | tf_op jit(solution)/shard_map/attend/pallas_call | solution.py:467
  80.2 78.3 %finish.1 = (f32[280,1120]{1,0:T(8,128)}, f32[280,1120]{1,0:T(8,128)}, bf16[2240,896]{1,0:T(8,128)(2,1)}) custom-call(f32[48,8,128]{2,1,0:T(8,128)} %get-tuple-element.17.r_0_, bf16[2,896,1120]{2,1,0:T(8,128)(2,1)} %get-tuple-element.18.r_1_, bf16[8,280,896]{2,1,0:T(8,128)(2,1)} %bitcast.22, bf16[8,280,896]{2,1,0:T(8,128)(2,1)} %bitcast.23, ...), custom_call_target="tpu_custom_call" | custom-call | tf_op jit(solution)/shard_map/finish/pallas_call | solution.py:747
  158.5 0.0 copy-start.1
  158.5 4.5 %copy.13 = bf16[1,896,2240]{1,2,0:T(8,128)(2,1)} copy(bf16[1,896,2240]{1,2,0:T(8,128)(2,1)} %bitcast.24) | data formatting | bytes 8028160
  163.0 0.0 copy-done.1
  163.0 0.0 copy-start
  163.0 1.0 copy.14
  164.1 0.7 copy-done
  164.8 1.0 copy.15
Async XLA Ops:
  158.5 4.5 %copy-start.1 = (f32[280,1120]{1,0:T(8,128)S(1)}, f32[280,1120]{1,0:T(8,128)}, u32[]{:S(2)}) copy-start(f32[280,1120]{1,0:T(8,128)} %get-tuple-element.33) | copy-start | bytes 3763204
  163.0 1.8 %copy-start = (f32[280,1120]{1,0:T(8,128)S(1)}, f32[280,1120]{1,0:T(8,128)}, u32[]{:S(2)}) copy-start(f32[280,1120]{1,0:T(8,128)} %get-tuple-element.34) | copy-start | bytes 3763204

commit v5 on v4

--- a/solution.py
+++ b/solution.py
@@ -183,7 +183,6 @@
             zs[k, p].start()
 
     seed0(0, 0, 1, 2, 3)
-    seed0(1, 0, 1)
     swap = remote(tok_ref, tok_out, tsem.at[0], tsem.at[1], partner)
     owns = [
         pltpu.make_async_copy(
@@ -205,19 +204,27 @@
         tup[:, at] = jnp.transpose(tin[at])
         return 0
 
-    lax.fori_loop(0, whole, flip, 0)
+    lax.fori_loop(0, 2, flip, 0)
+    across_in(0, ZM0, ZM1)
+    lax.fori_loop(2, 3, flip, 0)
+    arrive(0, L0, R1)
+    seed0(1, 0, 1)
+    lax.fori_loop(3, 4, flip, 0)
+    arrive(0, L1, R0)
+    seed0(1, 2, 3)
+    across_in(1, ZM0, ZM1)
+    lax.fori_loop(4, 5, flip, 0)
+    arrive(0, YL0, YR1)
+    across_in(0, ZN0, ZN1)
+    lax.fori_loop(5, 6, flip, 0)
+    arrive(0, O0, O1)
+    swap.start()
+    arrive(1, L0, R1)
+    lax.fori_loop(6, whole, flip, 0)
+    arrive(0, YR0, YL1)
+    arrive(1, L1, R0)
     at = pl.ds(whole * ROWS, rest)
     tup[:, at] = jnp.transpose(tin[at])
-    across_in(0, ZM0, ZM1)
-    across_in(1, ZM0, ZM1)
-    arrive(0, L0, R1)
-    seed0(1, 2, 3)
-    arrive(0, L1, R0, YL0, YR1)
-    swap.start()
-    arrive(1, L0, R1)
-    across_in(0, ZN0, ZN1)
-    arrive(0, O0, O1, YR0, YL1)
-    arrive(1, L1, R0)
     arrive(0, YO0, YO1)
     settled(0)
     for c in owns:
@@ -448,10 +455,18 @@
     )
     d_den = -dots * inv
     dnh, dnl = split(d_num)
-    feat = dot(jnp.concatenate([kvh, kvh], axis=1), jnp.concatenate([dnh, dnl], axis=0))
-    feat = feat + dot(kvl, dnh) + d_den * col
+    pair = jnp.concatenate([dnh, dnl], axis=0)
+    back = jnp.concatenate(
+        [
+            jnp.concatenate([kvh, kvh], axis=1),
+            jnp.concatenate([kvl, jnp.zeros_like(kvl)], axis=1),
+        ],
+        axis=0,
+    )
+    feat = dot(back, pair)
+    feat = feat[:LANE] + feat[LANE:] + d_den * col
     dq_ref[...] = jnp.where(q > 0, feat, 0.0).astype(BF)
-    gs = dot_r(q, jnp.concatenate([dnh, dnl], axis=0))
+    gs = dot_r(q, pair)
     gn = jnp.sum(d_den * q.astype(F32), axis=1, keepdims=True)
     put_state(
         part_ref,
@@ -488,7 +503,7 @@
 
 def finish_kernel(scale, tok_img, part_ref, kv_ref, tok_ref, tok2_ref, w_ref, ok_ref, ov_ref, dt_ref,
                   cat, dcat, dboth, kvb, sums, slots, gp, relay, final, comb, res1, relay2, final2,
-                  res2, zbuf, fin, wbuf, tbuf, ssem, rsem, lsem, csem, wsem, osem, tsem):
+                  res2, zbuf, fin, wbuf, tbuf, ssem, rsem, lsem, csem, wsem, osem, tsem, psem):
     s = Seat()
     core = s.core
     x_r, x_l, y_r, y_l = s.at(dx=1), s.at(dx=-1), s.at(dy=1), s.at(dy=-1)
@@ -601,7 +616,9 @@
         def _():
             j = xx
             d = (right1, left1)
-            copy(gp.at[h, nxt(me1, 2), j], relay.at[h, j], h, d[h]).start()
+            remote(
+                gp.at[h, nxt(me1, 2), j], relay.at[h, j], psem.at[0, h, dx], psem.at[1, h, dx], d[h]
+            ).start()
             if h == 1:
                 copy(gp.at[1, nxt(me1, 1), j], final.at[0, 1, j], 2, right1).start()
             else:
@@ -638,6 +655,14 @@
         add(comb.at[1], gp.at[1, nxt(me1, 3)], relay.at[1])
         copy(comb.at[1], final.at[1, 1], 5, left1).start()
 
+    def combine_piece(h, dx):
+        j = nxt(s.x, dx)
+        arrived(relay.at[h, j], psem.at[1, h, dx])
+        mine = gp[h, nxt(me1, (1, 3)[h]), j].astype(F32)
+        comb[h, j] = (mine + relay[h, j].astype(F32)).astype(BF)
+        dst = (final.at[0, 0, j], final.at[1, 1, j])[h]
+        copy(comb.at[h, j], dst, 4 + h, (right1, left1)[h]).start()
+
     for c in ld[1:]:
         c.wait()
     swap(0).wait()
@@ -649,15 +674,27 @@
     def _():
         combine()
 
-    shard(0, 0)
-    shard(1, 0)
-
     @pl.when(core == 1)
     def _():
-        combine()
-
-    for i, dst in enumerate(
-        (relay.at[0], relay.at[1], final.at[0, 1], final.at[1, 0], final.at[0, 0], final.at[1, 1])
+        for h, dx in ((0, 2), (1, 2), (1, 1), (0, 3)):
+            combine_piece(h, dx)
+
+    shard(0, 0)
+
+    @pl.when(core == 1)
+    def _():
+        for h, dx in ((0, 1), (1, 3)):
+            combine_piece(h, dx)
+
+    shard(1, 0)
+
+    @pl.when(core == 1)
+    def _():
+        for h, dx in ((0, 0), (1, 0)):
+            combine_piece(h, dx)
+
+    for i, dst in (
+        (2, final.at[0, 1]), (3, final.at[1, 0]), (4, final.at[0, 0]), (5, final.at[1, 1])
     ):
         pending.append(copy(dst, dst, i, right1))
 
@@ -729,6 +766,19 @@
         arrived(fin.at[1 - core, y], csem.at[k])
     for c in pending:
         c.wait_send()
+
+    @pl.when(core == 0)
+    def _():
+        for h in range(2):
+            copy(relay.at[h], relay.at[h], h, right1).wait_send()
+
+    @pl.when(core == 1)
+    def _():
+        for h in range(2):
+            for dx in range(4):
+                ref = relay.at[h, nxt(s.x, dx)]
+                remote(ref, ref, psem.at[0, h, dx], psem.at[1, h, dx], right1).wait_send()
+
     for i in (bands - 2, bands - 1):
         bands_out(i).wait()
     for ref, i in ((ok_ref, 0), (ov_ref, 1)):
@@ -771,6 +821,7 @@
             pltpu.VMEM((2, 2, BAND, width), BF),
             pltpu.VMEM((2, BAND, count), BF),
             DMA((24,)), DMA((20,)), DMA((3,)), DMA((4,)), DMA((5,)), DMA((5,)), DMA((4, 16)),
+            DMA((2, 2, 4)),
         ],
         compiler_params=params(5),
     )(part, kv, tok.reshape(8, rows, count), tok2.reshape(8, rows, count), w)

time: 166 us -> 170 us (1.024)
  Pallas kernels: 158 us -> 161 us
    pallas_call x1, Pallas kernels: 78.3 us -> 82.1 us  [finish(): pl.pallas_call(lambda *r: finish_kernel(scale, tok_img, *r), name='finish...]
where the time goes in v5:
time: 170 us; the launch traced here: 169 us
  Pallas kernels  161 us (95%)
  local copies, waits for them, and re-layouts  7.33 us (4%)
    pallas_call x1, Pallas kernels, finish(): pl.pallas_call(lambda *r: finish_kernel(scale, tok_img, *r), name='finish...  82.1 us
    pallas_call x1, Pallas kernels, gather(): pl.pallas_call(gather_kernel, name='gather', out_shape=(jax.ShapeDtypeStr...  67.5 us
    pallas_call x1, Pallas kernels, attend(): pl.pallas_call(lambda *r: attend_kernel(width, *r), name='attend', grid=(...  11.5 us
    unnamed x7, local copies, waits for them, and re-layouts  7.33 us

profile of v5, /device:TPU:1, one launch (start us, length us, event | category | flops | bytes accessed | tf_op | source)
XLA Modules:
  0.0 169.1 jit_solution(9711355812154404305)
XLA Ops:
  0.6 67.5 %gather.1 = (bf16[2,2240,1120]{2,1,0:T(8,128)(2,1)}, bf16[2240,896]{1,0:T(8,128)(2,1)}, bf16[2,896,1120]{2,1,0:T(8,128)(2,1)}, f32[48,8,128]{2,1,0:T(8,128)}) custom-call(bf16[280,1120]{1,0:T(8,128)(2,1)} %wk_ref.1, bf16[280,1120]{1,0:T(8,128)(2,1)} %wv_ref.1, bf16[2240,896]{1,0:T(8,128)(2,1)} %bitcast.21), custom_call_target="tpu_custom_call" | custom-call | tf_op jit(solution)/shard_map/gather/pallas_call | solution.py:328
  68.2 11.5 %attend.1 = (bf16[1120,896]{1,0:T(8,128)(2,1)}, bf16[1120,896]{1,0:T(8,128)(2,1)}, f32[48,8,128]{2,1,0:T(8,128)}) custom-call(bf16[1120,896]{1,0:T(8,128)(2,1)} %bitcast.25, bf16[1120,896]{1,0:T(8,128)(2,1)} %bitcast.26, f32[48,8,128]{2,1,0:T(8,128)} %get-tuple-element.15.r_2_), custom_call_target="tpu_custom_call" | custom-call | tf_op jit(solution)/shard_map/attend/pallas_call | solution.py:482
  79.6 82.1 %finish.1 = (f32[280,1120]{1,0:T(8,128)}, f32[280,1120]{1,0:T(8,128)}, bf16[2240,896]{1,0:T(8,128)(2,1)}) custom-call(f32[48,8,128]{2,1,0:T(8,128)} %get-tuple-element.17.r_0_, bf16[2,896,1120]{2,1,0:T(8,128)(2,1)} %get-tuple-element.18.r_1_, bf16[8,280,896]{2,1,0:T(8,128)(2,1)} %bitcast.22, bf16[8,280,896]{2,1,0:T(8,128)(2,1)} %bitcast.23, ...), custom_call_target="tpu_custom_call" | custom-call | tf_op jit(solution)/shard_map/finish/pallas_call | solution.py:797
  161.7 0.0 copy-start.1
  161.7 4.5 %copy.13 = bf16[1,896,2240]{1,2,0:T(8,128)(2,1)} copy(bf16[1,896,2240]{1,2,0:T(8,128)(2,1)} %bitcast.24) | data formatting | bytes 8028160
  166.2 0.0 copy-done.1
  166.2 0.0 copy-start
  166.2 1.0 copy.14
  167.3 0.7 copy-done
  168.0 1.0 copy.15
Async XLA Ops:
  161.7 4.5 %copy-start.1 = (f32[280,1120]{1,0:T(8,128)S(1)}, f32[280,1120]{1,0:T(8,128)}, u32[]{:S(2)}) copy-start(f32[280,1120]{1,0:T(8,128)} %get-tuple-element.33) | copy-start | bytes 3763204
  166.2 1.8 %copy-start = (f32[280,1120]{1,0:T(8,128)S(1)}, f32[280,1120]{1,0:T(8,128)}, u32[]{:S(2)}) copy-start(f32[280,1120]{1,0:T(8,128)} %get-tuple-element.34) | copy-start | bytes 3763204

commit v6 on v5

--- a/solution.py
+++ b/solution.py
@@ -16,11 +16,11 @@
 DMA = pltpu.SemaphoreType.DMA
 
 
-def params(cid=None, sem=None):
+def params(cid=None, sem=None, grant=VMEM_MAX):
     return pltpu.CompilerParams(
         collective_id=cid,
         has_side_effects=cid is not None,
-        vmem_limit_bytes=VMEM_MAX,
+        vmem_limit_bytes=grant,
         dimension_semantics=sem,
     )
 
@@ -503,7 +503,7 @@
 
 def finish_kernel(scale, tok_img, part_ref, kv_ref, tok_ref, tok2_ref, w_ref, ok_ref, ov_ref, dt_ref,
                   cat, dcat, dboth, kvb, sums, slots, gp, relay, final, comb, res1, relay2, final2,
-                  res2, zbuf, fin, wbuf, tbuf, ssem, rsem, lsem, csem, wsem, osem, tsem, psem):
+                  res2, zbuf, fin, wbuf, ssem, rsem, lsem, csem, wsem, tsem):
     s = Seat()
     core = s.core
     x_r, x_l, y_r, y_l = s.at(dx=1), s.at(dx=-1), s.at(dy=1), s.at(dy=-1)
@@ -589,24 +589,23 @@
     def nxt(v, k):
         return (v + k) % 4
 
-    def bands_out(i):
-        at = pl.ds(i * BAND, BAND)
-        return pltpu.make_async_copy(tbuf.at[i % 2], dt_ref.at[at], osem.at[i])
-
     def band(i):
         band_load(i).wait()
-        if i >= 2:
-            bands_out(i - 2).wait()
         both = wbuf.at[i % 2]
         v = dot_r(both[0], dboth[0]) + dot_r(both[1], dboth[1])
-        tbuf[i % 2] = v.astype(BF)
-        bands_out(i).start()
+        dt_ref[pl.ds(i * BAND, BAND)] = v.astype(BF)
         if i + 2 < bands:
             band_load(i + 2).start()
 
-    def shard(h, dx):
+    def shard(h, dx, first=False):
         xx = nxt(s.x, dx)
-        v = dot(cat[h * 4 + xx], dcat[...])
+        if first:
+            v = dot(cat[h * 4 + xx, :, lo], dcat[lo])
+            swap(0).wait()
+            swap(1).wait()
+            v = v + dot(cat[h * 4 + xx, :, up], dcat[up])
+        else:
+            v = dot(cat[h * 4 + xx], dcat[...])
         for y in range(4):
             c = xx * (1 - core) + y * core
             j = y * (1 - core) + xx * core
@@ -616,9 +615,7 @@
         def _():
             j = xx
             d = (right1, left1)
-            remote(
-                gp.at[h, nxt(me1, 2), j], relay.at[h, j], psem.at[0, h, dx], psem.at[1, h, dx], d[h]
-            ).start()
+            copy(gp.at[h, nxt(me1, 2), j], relay.at[h, j], h, d[h]).start()
             if h == 1:
                 copy(gp.at[1, nxt(me1, 1), j], final.at[0, 1, j], 2, right1).start()
             else:
@@ -655,46 +652,23 @@
         add(comb.at[1], gp.at[1, nxt(me1, 3)], relay.at[1])
         copy(comb.at[1], final.at[1, 1], 5, left1).start()
 
-    def combine_piece(h, dx):
-        j = nxt(s.x, dx)
-        arrived(relay.at[h, j], psem.at[1, h, dx])
-        mine = gp[h, nxt(me1, (1, 3)[h]), j].astype(F32)
-        comb[h, j] = (mine + relay[h, j].astype(F32)).astype(BF)
-        dst = (final.at[0, 0, j], final.at[1, 1, j])[h]
-        copy(comb.at[h, j], dst, 4 + h, (right1, left1)[h]).start()
-
     for c in ld[1:]:
         c.wait()
-    swap(0).wait()
-    swap(1).wait()
-    for h, dx in ((0, 2), (1, 2), (1, 1), (0, 3), (0, 1), (1, 3)):
-        shard(h, dx)
+    for h, dx in ((0, 2), (1, 2), (1, 1), (0, 3), (0, 1), (1, 3), (0, 0)):
+        shard(h, dx, (h, dx) == (0, 2))
 
     @pl.when(core == 0)
     def _():
         combine()
 
+    shard(1, 0)
+
     @pl.when(core == 1)
     def _():
-        for h, dx in ((0, 2), (1, 2), (1, 1), (0, 3)):
-            combine_piece(h, dx)
-
-    shard(0, 0)
-
-    @pl.when(core == 1)
-    def _():
-        for h, dx in ((0, 1), (1, 3)):
-            combine_piece(h, dx)
-
-    shard(1, 0)
-
-    @pl.when(core == 1)
-    def _():
-        for h, dx in ((0, 0), (1, 0)):
-            combine_piece(h, dx)
-
-    for i, dst in (
-        (2, final.at[0, 1]), (3, final.at[1, 0]), (4, final.at[0, 0]), (5, final.at[1, 1])
+        combine()
+
+    for i, dst in enumerate(
+        (relay.at[0], relay.at[1], final.at[0, 1], final.at[1, 0], final.at[0, 0], final.at[1, 1])
     ):
         pending.append(copy(dst, dst, i, right1))
 
@@ -766,21 +740,6 @@
         arrived(fin.at[1 - core, y], csem.at[k])
     for c in pending:
         c.wait_send()
-
-    @pl.when(core == 0)
-    def _():
-        for h in range(2):
-            copy(relay.at[h], relay.at[h], h, right1).wait_send()
-
-    @pl.when(core == 1)
-    def _():
-        for h in range(2):
-            for dx in range(4):
-                ref = relay.at[h, nxt(s.x, dx)]
-                remote(ref, ref, psem.at[0, h, dx], psem.at[1, h, dx], right1).wait_send()
-
-    for i in (bands - 2, bands - 1):
-        bands_out(i).wait()
     for ref, i in ((ok_ref, 0), (ov_ref, 1)):
         for y in range(3):
             ref[pl.ds(PIECE * y, PIECE)] = fin[i, y].astype(F32) * scale
@@ -797,10 +756,10 @@
     return pl.pallas_call(
         lambda *r: finish_kernel(scale, tok_img, *r),
         name="finish",
-        out_shape=(jax.ShapeDtypeStruct((rows, width), F32),) * 2
-        + (jax.ShapeDtypeStruct((depth, count), BF),),
+        out_shape=(pltpu.VMEM((rows, width), F32),) * 2
+        + (pltpu.VMEM((depth, count), BF),),
         in_specs=[vm] + [hbm] * 4,
-        out_specs=(vm, vm, hbm),
+        out_specs=(vm, vm, vm),
         scratch_shapes=[
             pltpu.VMEM((8, rows, 2 * count), BF),
             pltpu.VMEM((2 * count, width), BF),
@@ -819,11 +778,9 @@
             pltpu.VMEM((3,) + p, BF),
             pltpu.VMEM((2, 4) + p, BF),
             pltpu.VMEM((2, 2, BAND, width), BF),
-            pltpu.VMEM((2, BAND, count), BF),
-            DMA((24,)), DMA((20,)), DMA((3,)), DMA((4,)), DMA((5,)), DMA((5,)), DMA((4, 16)),
-            DMA((2, 2, 4)),
+            DMA((24,)), DMA((20,)), DMA((3,)), DMA((4,)), DMA((5,)), DMA((4, 16)),
         ],
-        compiler_params=params(5),
+        compiler_params=params(5, grant=52 * 1024 * 1024),
     )(part, kv, tok.reshape(8, rows, count), tok2.reshape(8, rows, count), w)
 
 

time: 170 us -> 160 us (0.941)
  Pallas kernels: 161 us -> 155 us
  local copies, waits for them, and re-layouts: 7.33 us -> 4.05 us
    pallas_call x1, Pallas kernels: 82.1 us -> 76.4 us  [finish(): pl.pallas_call(lambda *r: finish_kernel(scale, tok_img, *r), name='finish...]
    unnamed x7 -> x3, local copies, waits for them, and re-layouts: 7.33 us -> 4.05 us
where the time goes in v6:
time: 160 us
  Pallas kernels  155 us (97%)
  local copies, waits for them, and re-layouts  4.05 us (3%)
    pallas_call x1, Pallas kernels, finish(): pl.pallas_call(lambda *r: finish_kernel(scale, tok_img, *r), name='finish...  76.4 us
    pallas_call x1, Pallas kernels, gather(): pl.pallas_call(gather_kernel, name='gather', out_shape=(jax.ShapeDtypeStr...  67.5 us
    pallas_call x1, Pallas kernels, attend(): pl.pallas_call(lambda *r: attend_kernel(width, *r), name='attend', grid=(...  11.5 us
    unnamed x3, local copies, waits for them, and re-layouts  4.05 us

profile of v6, /device:TPU:1, one launch (start us, length us, event | category | flops | bytes accessed | tf_op | source)
XLA Modules:
  0.0 160.1 jit_solution(5114399834133865499)
XLA Ops:
  0.6 67.5 %gather.1 = (bf16[2,2240,1120]{2,1,0:T(8,128)(2,1)}, bf16[2240,896]{1,0:T(8,128)(2,1)}, bf16[2,896,1120]{2,1,0:T(8,128)(2,1)}, f32[48,8,128]{2,1,0:T(8,128)}) custom-call(bf16[280,1120]{1,0:T(8,128)(2,1)} %wk_ref.1, bf16[280,1120]{1,0:T(8,128)(2,1)} %wv_ref.1, bf16[2240,896]{1,0:T(8,128)(2,1)} %bitcast.22), custom_call_target="tpu_custom_call" | custom-call | tf_op jit(solution)/shard_map/gather/pallas_call | solution.py:328
  68.2 11.5 %attend.1 = (bf16[1120,896]{1,0:T(8,128)(2,1)}, bf16[1120,896]{1,0:T(8,128)(2,1)}, f32[48,8,128]{2,1,0:T(8,128)}) custom-call(bf16[1120,896]{1,0:T(8,128)(2,1)} %bitcast.25, bf16[1120,896]{1,0:T(8,128)(2,1)} %bitcast.26, f32[48,8,128]{2,1,0:T(8,128)} %get-tuple-element.15.r_2_), custom_call_target="tpu_custom_call" | custom-call | tf_op jit(solution)/shard_map/attend/pallas_call | solution.py:482
  79.6 76.4 %finish.1 = (f32[280,1120]{1,0:T(8,128)S(1)}, f32[280,1120]{1,0:T(8,128)S(1)}, bf16[2240,896]{1,0:T(8,128)(2,1)S(1)}) custom-call(f32[48,8,128]{2,1,0:T(8,128)} %get-tuple-element.17.r_0_, bf16[2,896,1120]{2,1,0:T(8,128)(2,1)} %get-tuple-element.18.r_1_, bf16[8,280,896]{2,1,0:T(8,128)(2,1)} %bitcast.23, bf16[8,280,896]{2,1,0:T(8,128)(2,1)} %bitcast.24, ...), custom_call_target="tpu_custom_call" | custom-call | tf_op jit(solution)/shard_map/finish/pallas_call | solution.py:756
  156.0 2.0 %copy.13 = bf16[1,896,2240]{1,2,0:T(8,128)(2,1)} copy(bf16[1,896,2240]{1,2,0:T(8,128)(2,1)S(1)} %bitcast.21) | data formatting | bytes 8028160
  158.0 1.0 copy.14
  159.0 1.0 copy.15

commit v7 on v6

--- a/solution.py
+++ b/solution.py
@@ -708,17 +708,22 @@
     arrived(final2.at[1, 1], rsem.at[11])
     res2[1] = plus(res1.at[1, me2], final2.at[0, 1], final2.at[1, 1])
 
-    go(res2.at[1 - s.zhi], zbuf.at[0], 12, across)
-    arrived(zbuf.at[0], rsem.at[12])
-    zbuf[2] = plus(res2.at[s.zhi], zbuf.at[0])
-    go(zbuf.at[2], zbuf.at[1], 13, beside)
-    arrived(zbuf.at[1], rsem.at[13])
+    a, b = pl.ds(0, CUT), pl.ds(CUT, width - CUT)
     mine = fin.at[core, s.y]
-    mine[...] = plus(zbuf.at[1], zbuf.at[2])
-
     yd, yu, yo = (s.y + 3) % 4, (s.y + 1) % 4, (s.y + 2) % 4
-    go(mine, mine, 14, y_r)
-    go(mine, mine, 15, y_l)
+    halves = ((a, 12, 13, 14, 15), (b, 24, 25, 26, 27))
+    for c, i, _, _, _ in halves:
+        go(res2.at[1 - s.zhi, :, c], zbuf.at[0, :, c], i, across)
+    for c, i, j, _, _ in halves:
+        arrived(zbuf.at[0, :, c], rsem.at[i])
+        zbuf[2, :, c] = plus(res2.at[s.zhi, :, c], zbuf.at[0, :, c])
+        go(zbuf.at[2, :, c], zbuf.at[1, :, c], j, beside)
+
+    for c, _, j, r, l in halves:
+        arrived(zbuf.at[1, :, c], rsem.at[j])
+        fin[core, s.y, :, c] = plus(zbuf.at[1, :, c], zbuf.at[2, :, c])
+        go(mine.at[:, c], mine.at[:, c], r, y_r)
+        go(mine.at[:, c], mine.at[:, c], l, y_l)
 
     def chip(ref, k):
         c = remote(ref, ref, ssem.at[k], csem.at[k - 18], partner)
@@ -726,13 +731,14 @@
         pending.append(c)
 
     chip(mine, 18)
-    a, b = pl.ds(0, CUT), pl.ds(CUT, mine.shape[1] - CUT)
-    arrived(fin.at[core, yd], rsem.at[14])
+    arrived(fin.at[core, yd, :, a], rsem.at[14])
     go(fin.at[core, yd, :, a], fin.at[core, yd, :, a], 16, y_r)
-    chip(fin.at[core, yd], 19)
-    arrived(fin.at[core, yu], rsem.at[15])
+    arrived(fin.at[core, yu, :, a], rsem.at[15])
+    arrived(fin.at[core, yu, :, b], rsem.at[27])
     go(fin.at[core, yu, :, b], fin.at[core, yu, :, b], 17, y_l)
     chip(fin.at[core, yu], 20)
+    arrived(fin.at[core, yd, :, b], rsem.at[26])
+    chip(fin.at[core, yd], 19)
     arrived(fin.at[core, yo, :, a], rsem.at[16])
     arrived(fin.at[core, yo, :, b], rsem.at[17])
     chip(fin.at[core, yo], 21)
@@ -778,7 +784,7 @@
             pltpu.VMEM((3,) + p, BF),
             pltpu.VMEM((2, 4) + p, BF),
             pltpu.VMEM((2, 2, BAND, width), BF),
-            DMA((24,)), DMA((20,)), DMA((3,)), DMA((4,)), DMA((5,)), DMA((4, 16)),
+            DMA((28,)), DMA((28,)), DMA((3,)), DMA((4,)), DMA((5,)), DMA((4, 16)),
         ],
         compiler_params=params(5, grant=52 * 1024 * 1024),
     )(part, kv, tok.reshape(8, rows, count), tok2.reshape(8, rows, count), w)

time: 160 us -> 159 us (level)
  no operation moved by 1% of the time
where the time goes in v7:
time: 159 us
  Pallas kernels  154 us (97%)
  local copies, waits for them, and re-layouts  4.05 us (3%)
    pallas_call x1, Pallas kernels, finish(): pl.pallas_call(lambda *r: finish_kernel(scale, tok_img, *r), name='finish...  74.9 us
    pallas_call x1, Pallas kernels, gather(): pl.pallas_call(gather_kernel, name='gather', out_shape=(jax.ShapeDtypeStr...  67.5 us
    pallas_call x1, Pallas kernels, attend(): pl.pallas_call(lambda *r: attend_kernel(width, *r), name='attend', grid=(...  11.5 us
    unnamed x3, local copies, waits for them, and re-layouts  4.05 us

profile of v7, /device:TPU:1, one launch (start us, length us, event | category | flops | bytes accessed | tf_op | source)
XLA Modules:
  0.0 158.6 jit_solution(14612647555953215566)
XLA Ops:
  0.6 67.5 %gather.1 = (bf16[2,2240,1120]{2,1,0:T(8,128)(2,1)}, bf16[2240,896]{1,0:T(8,128)(2,1)}, bf16[2,896,1120]{2,1,0:T(8,128)(2,1)}, f32[48,8,128]{2,1,0:T(8,128)}) custom-call(bf16[280,1120]{1,0:T(8,128)(2,1)} %wk_ref.1, bf16[280,1120]{1,0:T(8,128)(2,1)} %wv_ref.1, bf16[2240,896]{1,0:T(8,128)(2,1)} %bitcast.22), custom_call_target="tpu_custom_call" | custom-call | tf_op jit(solution)/shard_map/gather/pallas_call | solution.py:328
  68.2 11.5 %attend.1 = (bf16[1120,896]{1,0:T(8,128)(2,1)}, bf16[1120,896]{1,0:T(8,128)(2,1)}, f32[48,8,128]{2,1,0:T(8,128)}) custom-call(bf16[1120,896]{1,0:T(8,128)(2,1)} %bitcast.25, bf16[1120,896]{1,0:T(8,128)(2,1)} %bitcast.26, f32[48,8,128]{2,1,0:T(8,128)} %get-tuple-element.15.r_2_), custom_call_target="tpu_custom_call" | custom-call | tf_op jit(solution)/shard_map/attend/pallas_call | solution.py:482
  79.6 74.9 %finish.1 = (f32[280,1120]{1,0:T(8,128)S(1)}, f32[280,1120]{1,0:T(8,128)S(1)}, bf16[2240,896]{1,0:T(8,128)(2,1)S(1)}) custom-call(f32[48,8,128]{2,1,0:T(8,128)} %get-tuple-element.17.r_0_, bf16[2,896,1120]{2,1,0:T(8,128)(2,1)} %get-tuple-element.18.r_1_, bf16[8,280,896]{2,1,0:T(8,128)(2,1)} %bitcast.23, bf16[8,280,896]{2,1,0:T(8,128)(2,1)} %bitcast.24, ...), custom_call_target="tpu_custom_call" | custom-call | tf_op jit(solution)/shard_map/finish/pallas_call | solution.py:762
  154.5 2.0 %copy.13 = bf16[1,896,2240]{1,2,0:T(8,128)(2,1)} copy(bf16[1,896,2240]{1,2,0:T(8,128)(2,1)S(1)} %bitcast.21) | data formatting | bytes 8028160
  156.5 1.0 copy.14
  157.5 1.0 copy.15
